TPU v7x, 512 devices: a whole 4x8x8 slice. The times are simulated.
512 devices in a mesh: heads: 8 (over z), seq: 64 (over x, y, core).
Axes of the slice: x: 4, y: 8, z: 8, core: 2. Of those that a mesh axis runs over, the one named last changes fastest.
Arguments:
- queries: bfloat16 [32768, 4096], P('seq', 'heads'), may hold values from -6 to 6
- key_vectors: bfloat16 [32768, 4096], P('seq', 'heads'), may hold values from -6 to 6
- values: bfloat16 [32768, 4096], P('seq', 'heads'), may hold values from -40 to 40
- level_weights: float32 [16, 32, 32768], P(None, 'heads', 'seq'), may hold values from 0.1 to 1
- gate_branch: bfloat16 [32768, 4096], P(('seq', 'heads')), may hold values from -6 to 6
- norm_gain: float32 [4096], replicated, may hold values from 0.5 to 1.5
Outputs:
- normed: bfloat16 [32768, 4096], P(('seq', 'heads'))
All inputs are finite; a program needn't handle non-finite values.
Results may differ from a plain program's by a relative error of at most 0.008.
Values may be sent and summed in bfloat16 or wider, within the bound.
A program may use at most 64 MiB of HBM per device.

v0:
```python
import jax
import jax.numpy as jnp
from jax import lax
from jax.sharding import PartitionSpec as P

HEAD_DIM = 128
WINDOW = 512


EPSILON = 1e-06


def passed_along(value, axis, steps):
    count = lax.axis_size(axis)
    leading, last = (max(0, -steps), min(count, count - steps))
    return lax.ppermute(value, axis, [(source, source + steps) for source in range(leading, last)])


def from_partner(shard, axis, apart):
    return lax.ppermute(shard, axis, [(i, i ^ 1 << apart) for i in range(lax.axis_size(axis))])


def bit_count(numbers, width_bits):
    lengths = jnp.zeros(numbers.shape, jnp.int32)
    for shift_bit in range(width_bits):
        lengths = lengths + (numbers >> shift_bit > 0).astype(jnp.int32)
    return lengths


def level_scale(levels):
    return jnp.exp2(-0.5 * jnp.maximum(levels - 1, 0).astype(jnp.float32))


def local(queries, key_vectors, values, level_weights, gate_branch, norm_gain):
    tok_rows = queries.shape[0]
    head_groups = queries.shape[1] // HEAD_DIM
    near_count = tok_rows.bit_length()
    far_count = level_weights.shape[0] - near_count
    score_scale = HEAD_DIM ** (-0.5)
    seq_place = lax.axis_index("seq")
    first_token = seq_place * tok_rows
    key_pieces = [key_vectors]
    value_pieces = [values]
    moved_keys, moved_values = passed_along((key_vectors, values), "seq", 1)
    key_pieces.insert(0, moved_keys)
    value_pieces.insert(0, moved_values)
    context_keys = jnp.concatenate(key_pieces, axis=0).reshape(-1, head_groups, HEAD_DIM)
    context_values = jnp.concatenate(value_pieces, axis=0).reshape(-1, head_groups, HEAD_DIM)
    query_heads = queries.reshape(tok_rows, head_groups, HEAD_DIM)
    key_heads = key_vectors.reshape(tok_rows, head_groups, HEAD_DIM)
    value_heads = values.reshape(tok_rows, head_groups, HEAD_DIM)
    states = jnp.einsum(
        "khd,khe->hde", key_heads, value_heads, preferred_element_type=jnp.float32
    ).astype(jnp.bfloat16)
    running = states.astype(jnp.float32)
    bucket_list = []
    for level_id in range(far_count):
        partner = from_partner(running, "seq", level_id)
        bucket_list.append(partner * (seq_place >> level_id & 1).astype(jnp.float32))
        running = running + partner
    buckets = jnp.stack(bucket_list, axis=0)
    bucket_half = buckets.astype(jnp.bfloat16)
    far_proj = jnp.einsum(
        "qhd,jhde->jqhe", query_heads, bucket_half, preferred_element_type=jnp.float32
    )
    far_scale = level_scale(near_count + jnp.arange(far_count, dtype=jnp.int32)) * score_scale
    far_coef = level_weights[near_count:] * far_scale[:, None, None]
    far_out = jnp.sum(jnp.transpose(far_coef, (0, 2, 1))[:, :, :, None] * far_proj, axis=0)
    positions = jnp.arange(tok_rows, dtype=jnp.int32)
    level_table = bit_count(positions[:, None] ^ positions[None, :], near_count)
    causal = positions[:, None] >= positions[None, :]
    near_scale = level_scale(jnp.arange(near_count, dtype=jnp.int32))
    query_block = min(tok_rows, 512)
    key_low = min(0, WINDOW)
    key_high = WINDOW + query_block
    scores = (
        jnp.einsum("qhd,khd->hqk", query_heads, context_keys, preferred_element_type=jnp.float32)
        * score_scale
    )
    query_pos = 0 + jnp.arange(query_block, dtype=jnp.int32)
    key_pos = key_low - WINDOW + jnp.arange(key_high - key_low, dtype=jnp.int32)
    pos_gap = query_pos[:, None] - key_pos[None, :]
    in_window = (pos_gap >= 0) & (pos_gap < WINDOW) & (key_pos + first_token >= 0)[None, :]
    row_max = jnp.max(jnp.where(in_window[None], scores, -jnp.inf), axis=2, keepdims=True)
    exp_scores = jnp.where(in_window[None], jnp.exp(scores - row_max), 0.0)
    weights = (exp_scores / jnp.sum(exp_scores, axis=2, keepdims=True)).astype(jnp.bfloat16)
    windowed = jnp.einsum(
        "hqk,khd->qhd", weights, context_values, preferred_element_type=jnp.float32
    )
    level_mix = jnp.zeros((head_groups, query_block, query_block), jnp.float32)
    for level_id in range(near_count):
        row_weights = level_weights[level_id] * near_scale[level_id]
        level_mix = level_mix + jnp.where(
            level_table[None] == level_id, row_weights[:, :, None], 0.0
        )
    level_mix = jnp.where(causal[None], level_mix, 0.0)
    own_scores = scores[:, :, WINDOW - key_low :]
    near_weights = (own_scores * level_mix).astype(jnp.bfloat16)
    near_out = jnp.einsum(
        "hqk,khd->qhd",
        near_weights,
        context_values[WINDOW : WINDOW + query_block],
        preferred_element_type=jnp.float32,
    )
    pieces = windowed + near_out + far_out
    mixed = pieces.reshape(tok_rows, head_groups * HEAD_DIM).astype(jnp.bfloat16)
    token_rows = lax.all_to_all(mixed, "heads", split_axis=0, concat_axis=1, tiled=True)
    gated = token_rows.astype(jnp.float32) * jax.nn.silu(gate_branch.astype(jnp.float32))
    mean_square = jnp.mean(gated * gated, axis=1, keepdims=True)
    return (norm_gain * gated * lax.rsqrt(mean_square + EPSILON)).astype(jnp.bfloat16)


def solution(mesh):
    return jax.shard_map(
        local,
        mesh=mesh,
        in_specs=(
            P("seq", "heads"),
            P("seq", "heads"),
            P("seq", "heads"),
            P(None, "heads", "seq"),
            P(("seq", "heads"), None),
            P(),
        ),
        out_specs=P(("seq", "heads"), None),
        check_vma=False,
    )
```

profile of v0, /device:TPU:6, one launch (start us, length us, event | category | flops | bytes accessed | tf_op | source)
XLA Modules:
  0.0 136.2 jit_solution(9132331737737762646)
XLA Ops:
  0.0 1.3 copy.35
  1.3 1.9 %collective-permute-start.1 = (bf16[512,512]{0,1:T(8,128)(2,1)S(1)}, bf16[512,512]{0,1:T(8,128)(2,1)S(1)}, u32[]{:S(2)}, u32[]{:S(2)}) collective-permute-start(bf16[512,512]{0,1:T(8,128)(2,1)S(1)} %copy.35), channel_id=1, source_target_pairs={{0,1},{1,2},{2,3},{3,4},{4,5},{5,6},{6,7},{7,8},{8,9},{9,10},{10,1... | collective-permute-start | bytes 1572872 | tf_op jit(solution)/shard_map/ppermute | solution.py:16
  3.2 3.6 %collective-permute-start = (bf16[512,512]{1,0:T(8,128)(2,1)}, bf16[512,512]{1,0:T(8,128)(2,1)}, u32[]{:S(2)}, u32[]{:S(2)}) collective-permute-start(bf16[512,512]{1,0:T(8,128)(2,1)} %param.8), channel_id=1, source_target_pairs={{0,1},{1,2},{2,3},{3,4},{4,5},{5,6},{6,7},{7,8},{8,9},{9,10},{10,1... | collective-permute-start | bytes 1572872 | tf_op jit(solution)/shard_map/ppermute | solution.py:16
  6.8 1.3 fusion.22
  8.2 1.9 %collective-permute-start.2 = (f32[4,128,128]{2,1,0:T(8,128)S(1)}, f32[4,128,128]{2,1,0:T(8,128)S(1)}, u32[]{:S(2)}, u32[]{:S(2)}) collective-permute-start(f32[4,128,128]{2,1,0:T(8,128)S(1)} %fusion.22), channel_id=1, source_target_pairs={{0,1},{1,0},{2,3},{3,2},{4,5},{5,4},{6,7},{7,6},{8,9},{9,8},{10,11... | collective-permute-start | bytes 786440 | tf_op jit(solution)/shard_map/ppermute | solution.py:20
  10.1 1.5 %iota_compare_fusion = (pred[512,512]{0,1:T(8,128)(4,1)S(1)}, pred[512,512]{0,1:T(8,128)(4,1)S(1)}) fusion(), kind=kLoop, calls=%fused_computation.49 | loop fusion | flops 11010048 | bytes 524288 | tf_op jit(solution)/shard_map/ge | solution.py:71
  11.6 1.6 %broadcast_compare_fusion.1 = (pred[512,512]{0,1:T(8,128)(4,1)S(1)}, pred[512,512]{0,1:T(8,128)(4,1)S(1)}) fusion(), kind=kLoop, calls=%fused_computation.57 | loop fusion | flops 11010048 | bytes 524288 | tf_op jit(solution)/shard_map/eq | solution.py:94
  13.2 2.3 %broadcast_compare_fusion.3 = (pred[512,512]{0,1:T(8,128)(4,1)S(1)}, pred[512,512]{0,1:T(8,128)(4,1)}) fusion(), kind=kLoop, calls=%fused_computation.59 | loop fusion | flops 11010048 | bytes 524288 | tf_op jit(solution)/shard_map/eq | solution.py:94
  15.5 2.4 %broadcast_compare_fusion.5 = (pred[512,512]{0,1:T(8,128)(4,1)}, pred[512,512]{0,1:T(8,128)(4,1)}) fusion(), kind=kLoop, calls=%fused_computation.61 | loop fusion | flops 11010048 | bytes 524288 | tf_op jit(solution)/shard_map/eq | solution.py:94
  17.9 2.4 %broadcast_compare_fusion.7 = (pred[512,512]{0,1:T(8,128)(4,1)}, pred[512,512]{0,1:T(8,128)(4,1)}) fusion(), kind=kLoop, calls=%fused_computation.63 | loop fusion | flops 11010048 | bytes 524288 | tf_op jit(solution)/shard_map/eq | solution.py:94
  20.3 2.1 %broadcast_compare_fusion.9 = pred[512,512]{0,1:T(8,128)(4,1)} fusion(), kind=kLoop, calls=%fused_computation.65 | loop fusion | flops 10747904 | bytes 262144 | tf_op jit(solution)/shard_map/eq | solution.py:94
  22.5 0.7 fusion.49
  23.1 1.9 %multiply_bitcast_fusion.2 = f32[4,512]{1,0:T(4,128)} fusion(f32[16,4,512]{2,1,0:T(4,128)} %param.9, f32[]{:T(128)} %bitcast.22), kind=kLoop, calls=%fused_computation.87 | loop fusion | flops 2048 | bytes 16388 | tf_op jit(solution)/shard_map/mul | solution.py:92
  25.0 0.9 multiply_bitcast_fusion.1
  25.9 6.9 %multiply_bitcast_fusion.11 = (f32[4,512]{1,0:T(4,128)S(1)}, f32[4,512]{1,0:T(4,128)S(1)}, f32[4,512]{1,0:T(4,128)S(1)}, f32[4,512]{1,0:T(4,128)}, f32[4,512]{1,...) fusion(f32[16,4,512]{2,1,0:T(4,128)} %param.9, f32[]{:T(128)} %bitcast.4, ...), kind=kLoop, calls=%fused_computation.96 | loop fusion | flops 18432 | bytes 147492 | tf_op jit(solution)/shard_map/mul | solution.py:92
  32.8 0.9 reshape.325
  33.7 0.9 fusion.12
  34.7 3.7 %collective-permute-start.3 = (f32[4,128,128]{2,1,0:T(8,128)S(1)}, f32[4,128,128]{2,1,0:T(8,128)S(1)}, u32[]{:S(2)}, u32[]{:S(2)}) collective-permute-start(f32[4,128,128]{2,1,0:T(8,128)S(1)} %add.589), channel_id=1, source_target_pairs={{0,2},{1,3},{2,0},{3,1},{4,6},{5,7},{6,4},{7,5},{8,10},{9,11},{10,... | collective-permute-start | bytes 786440 | tf_op jit(solution)/shard_map/ppermute | solution.py:20
  38.4 0.1 pad_maximum_fusion.1
  38.6 0.0 copy-start.2
  38.7 1.3 multiply_bitcast_fusion
  40.0 5.3 %collective-permute-done.3 = f32[4,128,128]{2,1,0:T(8,128)S(1)} collective-permute-done((f32[4,128,128]{2,1,0:T(8,128)S(1)}, f32[4,128,128]{2,1,0:T(8,128)S(1)}, u32[]{:S(2)}, u32[]{:S(2)}) %collective-permute-start.3) | collective-permute-done | bytes 262176 | tf_op jit(solution)/shard_map/ppermute | solution.py:20
  45.4 5.5 %collective-permute-start.4 = (f32[4,128,128]{2,1,0:T(8,128)S(1)}, f32[4,128,128]{2,1,0:T(8,128)S(1)}, u32[]{:S(2)}, u32[]{:S(2)}) collective-permute-start(f32[4,128,128]{2,1,0:T(8,128)S(1)} %add.590), channel_id=1, source_target_pairs={{0,4},{1,5},{2,6},{3,7},{4,0},{5,1},{6,2},{7,3},{8,12},{9,13},{10,... | collective-permute-start | bytes 786440 | tf_op jit(solution)/shard_map/ppermute | solution.py:20
  51.1 6.4 %fusion.15 = f32[512,4,128]{0,2,1:T(8,128)} fusion(f32[4,512,1024]{1,2,0:T(8,128)S(1)} %multiply_bitcast_fusion, f32[4,512]{1,0:T(4,128)S(1)} %copy-done.17, f32[4,512]{1,0:T(4,128)S(1)} %get-tuple-element.6, f32[4,512]{1,0:T(4,128)S(1)} %get-tuple-element.7, f32[4,512]{1,0:T(4,128)S(1)} %copy-done.11, f32[4,512]{1,0:T(4,128)S(1)} %copy-done.12, ...), kind=kOutput, calls=%fused_computation.19 | convolution fusion | flops 291504128 | bytes 8732672 | tf_op jit(solution)/shard_map/hqk,khd->qhd/dot_general | solution.py:99
  57.4 5.4 %collective-permute-done.4 = f32[4,128,128]{2,1,0:T(8,128)S(1)} collective-permute-done((f32[4,128,128]{2,1,0:T(8,128)S(1)}, f32[4,128,128]{2,1,0:T(8,128)S(1)}, u32[]{:S(2)}, u32[]{:S(2)}) %collective-permute-start.4) | collective-permute-done | bytes 262176 | tf_op jit(solution)/shard_map/ppermute | solution.py:20
  62.9 5.5 %collective-permute-start.5 = (f32[4,128,128]{2,1,0:T(8,128)S(1)}, f32[4,128,128]{2,1,0:T(8,128)S(1)}, u32[]{:S(2)}, u32[]{:S(2)}) collective-permute-start(f32[4,128,128]{2,1,0:T(8,128)S(1)} %add.591), channel_id=1, source_target_pairs={{0,8},{1,9},{2,10},{3,11},{4,12},{5,13},{6,14},{7,15},{8,0},{9,1},... | collective-permute-start | bytes 786440 | tf_op jit(solution)/shard_map/ppermute | solution.py:20
  68.5 5.7 %fusion.50 = (f32[4,512]{1,0:T(4,128)S(1)}, f32[4,512,1024]{1,2,0:T(8,128)}) fusion(f32[4,512,1024]{1,2,0:T(8,128)S(1)} %multiply_bitcast_fusion, pred[512,1024]{0,1:T(8,128)(4,1)S(1)} %fusion.12), kind=kOutput, calls=%fused_computation.105 | output fusion | flops 8389631 | bytes 17309696 | tf_op jit(solution)/shard_map/sub | solution.py:85
  74.3 7.6 %collective-permute-done.5 = f32[4,128,128]{2,1,0:T(8,128)S(1)} collective-permute-done((f32[4,128,128]{2,1,0:T(8,128)S(1)}, f32[4,128,128]{2,1,0:T(8,128)S(1)}, u32[]{:S(2)}, u32[]{:S(2)}) %collective-permute-start.5) | collective-permute-done | bytes 262176 | tf_op jit(solution)/shard_map/ppermute | solution.py:20
  81.9 2.7 %collective-permute-start.6 = (f32[4,128,128]{2,1,0:T(8,128)S(1)}, f32[4,128,128]{2,1,0:T(8,128)S(1)}, u32[]{:S(2)}, u32[]{:S(2)}) collective-permute-start(f32[4,128,128]{2,1,0:T(8,128)S(1)} %add.592), channel_id=1, source_target_pairs={{0,16},{1,17},{2,18},{3,19},{4,20},{5,21},{6,22},{7,23},{8,24},{9,... | collective-permute-start | bytes 786440 | tf_op jit(solution)/shard_map/ppermute | solution.py:20
  84.7 1.1 pad_maximum_fusion
  85.8 0.5 copy.34
  86.4 0.7 fusion.40
  87.0 4.2 %collective-permute-done.6 = f32[4,128,128]{2,1,0:T(8,128)S(1)} collective-permute-done((f32[4,128,128]{2,1,0:T(8,128)S(1)}, f32[4,128,128]{2,1,0:T(8,128)S(1)}, u32[]{:S(2)}, u32[]{:S(2)}) %collective-permute-start.6) | collective-permute-done | bytes 262176 | tf_op jit(solution)/shard_map/ppermute | solution.py:20
  91.3 3.8 %collective-permute-start.7 = (f32[4,128,128]{2,1,0:T(8,128)S(1)}, f32[4,128,128]{2,1,0:T(8,128)S(1)}, u32[]{:S(2)}, u32[]{:S(2)}) collective-permute-start(f32[4,128,128]{2,1,0:T(8,128)S(1)} %add.593), channel_id=1, source_target_pairs={{0,32},{1,33},{2,34},{3,35},{4,36},{5,37},{6,38},{7,39},{8,40},{9,... | collective-permute-start | bytes 786440 | tf_op jit(solution)/shard_map/ppermute | solution.py:20
  95.0 0.7 fusion.42
  95.7 0.7 fusion.44
  96.4 4.8 %collective-permute-done.7 = f32[4,128,128]{2,1,0:T(8,128)S(1)} collective-permute-done((f32[4,128,128]{2,1,0:T(8,128)S(1)}, f32[4,128,128]{2,1,0:T(8,128)S(1)}, u32[]{:S(2)}, u32[]{:S(2)}) %collective-permute-start.7) | collective-permute-done | bytes 262176 | tf_op jit(solution)/shard_map/ppermute | solution.py:20
  101.2 0.7 fusion.46
  101.9 2.4 %fusion.2 = f32[512,4,128]{0,2,1:T(8,128)S(1)} fusion(f32[6,512,4]{1,0,2:T(8,128)S(1)} %copy.43, bf16[6,4,128,128]{3,2,1,0:T(8,128)(2,1)} %fusion.46, bf16[512,4,128,1]{2,1,0,3:T(4,128)(2,1)} %bitcast.107), kind=kOutput, calls=%fused_computation.7 | convolution fusion | flops 405536768 | bytes 2408448 | tf_op jit(solution)/shard_map/qhd,jhde->jqhe/dot_general | solution.py:63
  104.3 4.2 %fusion.21 = bf16[512,4,128]{0,2,1:T(8,128)(2,1)S(1)} fusion(f32[512,4,128]{0,2,1:T(8,128)S(1)} %fusion.2, f32[512,4,128]{0,2,1:T(8,128)S(1)} %copy-done.18, bf16[1024,4,128]{0,2,1:T(8,128)(2,1)S(1)} %bitcast.106, f32[4,512,1024]{1,2,0:T(8,128)} %get-tuple-element.25, f32[4,512]{1,0:T(4,128)S(1)} %get-tuple-element.24), kind=kOutput, calls=%fused_computation.25 | convolution fusion | flops 541851648 | bytes 12066816 | tf_op jit(solution)/shard_map/hqk,khd->qhd/dot_general | solution.py:87
  108.5 0.0 copy-start.1
  108.6 0.3 copy.48
  108.9 0.2 convert_element_type.606
  109.1 25.2 %all_to_all.10 = bf16[8,64,512]{2,1,0:T(8,128)(2,1)S(1)} all-to-all(bf16[8,64,512]{2,1,0:T(8,128)(2,1)S(1)} %convert_element_type.606), channel_id=1, replica_groups=mesh['heads'=8,'seq'=64] {'heads'}, dimensions={0} | all-to-all | bytes 1048576 | tf_op jit(solution)/shard_map/all_to_all | solution.py:107
  134.3 0.1 convert_bitcast_fusion
  134.5 0.1 copy.62
  134.6 0.4 multiply_reduce_fusion
  135.0 1.2 multiply_convert_fusion
  (52 shorter events, 0.4 us)
Async XLA Ops:
  0.0 32.8 %copy-start = (bf16[512,512]{1,0:T(8,128)(2,1)S(1)}, bf16[512,512]{1,0:T(8,128)(2,1)}, u32[]{:S(2)}) copy-start(bf16[512,512]{1,0:T(8,128)(2,1)} %param.6) | copy-start | bytes 1572868
  1.3 37.1 %collective-permute-start.1 = (bf16[512,512]{0,1:T(8,128)(2,1)S(1)}, bf16[512,512]{0,1:T(8,128)(2,1)S(1)}, u32[]{:S(2)}, u32[]{:S(2)}) collective-permute-start(bf16[512,512]{0,1:T(8,128)(2,1)S(1)} %copy.35), channel_id=1, source_target_pairs={{0,1},{1,2},{2,3},{3,4},{4,5},{5,6},{6,7},{7,8},{8,9},{9,10},{10,1... | collective-permute-start | bytes 1572872 | tf_op jit(solution)/shard_map/ppermute | solution.py:16
  3.2 81.4 %collective-permute-start = (bf16[512,512]{1,0:T(8,128)(2,1)}, bf16[512,512]{1,0:T(8,128)(2,1)}, u32[]{:S(2)}, u32[]{:S(2)}) collective-permute-start(bf16[512,512]{1,0:T(8,128)(2,1)} %param.8), channel_id=1, source_target_pairs={{0,1},{1,2},{2,3},{3,4},{4,5},{5,6},{6,7},{7,8},{8,9},{9,10},{10,1... | collective-permute-start | bytes 1572872 | tf_op jit(solution)/shard_map/ppermute | solution.py:16
  8.2 26.5 %collective-permute-start.2 = (f32[4,128,128]{2,1,0:T(8,128)S(1)}, f32[4,128,128]{2,1,0:T(8,128)S(1)}, u32[]{:S(2)}, u32[]{:S(2)}) collective-permute-start(f32[4,128,128]{2,1,0:T(8,128)S(1)} %fusion.22), channel_id=1, source_target_pairs={{0,1},{1,0},{2,3},{3,2},{4,5},{5,4},{6,7},{7,6},{8,9},{9,8},{10,11... | collective-permute-start | bytes 786440 | tf_op jit(solution)/shard_map/ppermute | solution.py:20
  34.7 10.6 %collective-permute-start.3 = (f32[4,128,128]{2,1,0:T(8,128)S(1)}, f32[4,128,128]{2,1,0:T(8,128)S(1)}, u32[]{:S(2)}, u32[]{:S(2)}) collective-permute-start(f32[4,128,128]{2,1,0:T(8,128)S(1)} %add.589), channel_id=1, source_target_pairs={{0,2},{1,3},{2,0},{3,1},{4,6},{5,7},{6,4},{7,5},{8,10},{9,11},{10,... | collective-permute-start | bytes 786440 | tf_op jit(solution)/shard_map/ppermute | solution.py:20
  38.6 12.4 %copy-start.2 = (bf16[512,512]{1,0:T(8,128)(2,1)S(1)}, bf16[512,512]{1,0:T(8,128)(2,1)}, u32[]{:S(2)}) copy-start(bf16[512,512]{1,0:T(8,128)(2,1)} %param.8) | copy-start | bytes 1572868
  38.6 12.4 %copy-start.3 = (pred[512,512]{0,1:T(8,128)(4,1)S(1)}, pred[512,512]{0,1:T(8,128)(4,1)}, u32[]{:S(2)}) copy-start(pred[512,512]{0,1:T(8,128)(4,1)} %get-tuple-element.31) | copy-start | bytes 786436
  38.6 12.4 %copy-start.4 = (pred[512,512]{0,1:T(8,128)(4,1)S(1)}, pred[512,512]{0,1:T(8,128)(4,1)}, u32[]{:S(2)}) copy-start(pred[512,512]{0,1:T(8,128)(4,1)} %get-tuple-element.32) | copy-start | bytes 786436
  38.6 12.4 %copy-start.5 = (pred[512,512]{0,1:T(8,128)(4,1)S(1)}, pred[512,512]{0,1:T(8,128)(4,1)}, u32[]{:S(2)}) copy-start(pred[512,512]{0,1:T(8,128)(4,1)} %get-tuple-element.33) | copy-start | bytes 786436
  38.6 12.4 %copy-start.6 = (pred[512,512]{0,1:T(8,128)(4,1)S(1)}, pred[512,512]{0,1:T(8,128)(4,1)}, u32[]{:S(2)}) copy-start(pred[512,512]{0,1:T(8,128)(4,1)} %get-tuple-element.34) | copy-start | bytes 786436
  38.6 12.4 %copy-start.7 = (pred[512,512]{0,1:T(8,128)(4,1)S(1)}, pred[512,512]{0,1:T(8,128)(4,1)}, u32[]{:S(2)}) copy-start(pred[512,512]{0,1:T(8,128)(4,1)} %get-tuple-element.35) | copy-start | bytes 786436
  38.6 12.4 %copy-start.8 = (pred[512,512]{0,1:T(8,128)(4,1)S(1)}, pred[512,512]{0,1:T(8,128)(4,1)}, u32[]{:S(2)}) copy-start(pred[512,512]{0,1:T(8,128)(4,1)} %broadcast_compare_fusion.9) | copy-start | bytes 786436
  38.6 12.4 %copy-start.11 = (f32[4,512]{1,0:T(4,128)S(1)}, f32[4,512]{1,0:T(4,128)}, u32[]{:S(2)}) copy-start(f32[4,512]{1,0:T(4,128)} %get-tuple-element.8) | copy-start | bytes 24580
  38.6 12.4 %copy-start.12 = (f32[4,512]{1,0:T(4,128)S(1)}, f32[4,512]{1,0:T(4,128)}, u32[]{:S(2)}) copy-start(f32[4,512]{1,0:T(4,128)} %get-tuple-element.9) | copy-start | bytes 24580
  38.6 12.4 %copy-start.13 = (f32[4,512]{1,0:T(4,128)S(1)}, f32[4,512]{1,0:T(4,128)}, u32[]{:S(2)}) copy-start(f32[4,512]{1,0:T(4,128)} %get-tuple-element.10) | copy-start | bytes 24580
  38.7 12.4 %copy-start.14 = (f32[4,512]{1,0:T(4,128)S(1)}, f32[4,512]{1,0:T(4,128)}, u32[]{:S(2)}) copy-start(f32[4,512]{1,0:T(4,128)} %get-tuple-element.11) | copy-start | bytes 24580
  38.7 12.4 %copy-start.15 = (f32[4,512]{1,0:T(4,128)S(1)}, f32[4,512]{1,0:T(4,128)}, u32[]{:S(2)}) copy-start(f32[4,512]{1,0:T(4,128)} %get-tuple-element.12) | copy-start | bytes 24580
  38.7 12.4 %copy-start.16 = (f32[4,512]{1,0:T(4,128)S(1)}, f32[4,512]{1,0:T(4,128)}, u32[]{:S(2)}) copy-start(f32[4,512]{1,0:T(4,128)} %get-tuple-element.13) | copy-start | bytes 24580
  38.7 12.4 %copy-start.17 = (f32[4,512]{1,0:T(4,128)S(1)}, f32[4,512]{1,0:T(4,128)}, u32[]{:S(2)}) copy-start(f32[4,512]{1,0:T(4,128)} %multiply_bitcast_fusion.2) | copy-start | bytes 24580
  45.4 17.5 %collective-permute-start.4 = (f32[4,128,128]{2,1,0:T(8,128)S(1)}, f32[4,128,128]{2,1,0:T(8,128)S(1)}, u32[]{:S(2)}, u32[]{:S(2)}) collective-permute-start(f32[4,128,128]{2,1,0:T(8,128)S(1)} %add.590), channel_id=1, source_target_pairs={{0,4},{1,5},{2,6},{3,7},{4,0},{5,1},{6,2},{7,3},{8,12},{9,13},{10,... | collective-permute-start | bytes 786440 | tf_op jit(solution)/shard_map/ppermute | solution.py:20
  62.9 19.0 %collective-permute-start.5 = (f32[4,128,128]{2,1,0:T(8,128)S(1)}, f32[4,128,128]{2,1,0:T(8,128)S(1)}, u32[]{:S(2)}, u32[]{:S(2)}) collective-permute-start(f32[4,128,128]{2,1,0:T(8,128)S(1)} %add.591), channel_id=1, source_target_pairs={{0,8},{1,9},{2,10},{3,11},{4,12},{5,13},{6,14},{7,15},{8,0},{9,1},... | collective-permute-start | bytes 786440 | tf_op jit(solution)/shard_map/ppermute | solution.py:20
  74.2 10.4 %copy-start.9 = (bf16[6,4,128,128]{3,2,1,0:T(8,128)(2,1)}, bf16[6,4,128,128]{3,2,1,0:T(8,128)(2,1)S(1)}, u32[]{:S(2)}) copy-start(bf16[6,4,128,128]{3,2,1,0:T(8,128)(2,1)S(1)} %fusion.38) | copy-start | bytes 2359300
  81.9 9.3 %collective-permute-start.6 = (f32[4,128,128]{2,1,0:T(8,128)S(1)}, f32[4,128,128]{2,1,0:T(8,128)S(1)}, u32[]{:S(2)}, u32[]{:S(2)}) collective-permute-start(f32[4,128,128]{2,1,0:T(8,128)S(1)} %add.592), channel_id=1, source_target_pairs={{0,16},{1,17},{2,18},{3,19},{4,20},{5,21},{6,22},{7,23},{8,24},{9,... | collective-permute-start | bytes 786440 | tf_op jit(solution)/shard_map/ppermute | solution.py:20
  86.4 17.9 %copy-start.18 = (f32[512,4,128]{0,2,1:T(8,128)S(1)}, f32[512,4,128]{0,2,1:T(8,128)}, u32[]{:S(2)}) copy-start(f32[512,4,128]{0,2,1:T(8,128)} %fusion.15) | copy-start | bytes 3145732
  91.3 9.9 %collective-permute-start.7 = (f32[4,128,128]{2,1,0:T(8,128)S(1)}, f32[4,128,128]{2,1,0:T(8,128)S(1)}, u32[]{:S(2)}, u32[]{:S(2)}) collective-permute-start(f32[4,128,128]{2,1,0:T(8,128)S(1)} %add.593), channel_id=1, source_target_pairs={{0,32},{1,33},{2,34},{3,35},{4,36},{5,37},{6,38},{7,39},{8,40},{9,... | collective-permute-start | bytes 786440 | tf_op jit(solution)/shard_map/ppermute | solution.py:20
  108.5 26.0 %copy-start.1 = (bf16[64,4096]{1,0:T(8,128)(2,1)S(1)}, bf16[64,4096]{1,0:T(8,128)(2,1)}, u32[]{:S(2)}) copy-start(bf16[64,4096]{1,0:T(8,128)(2,1)} %param.10) | copy-start | bytes 1572868
  108.5 26.5 %copy-start.10 = (f32[4096]{0:T(1024)S(1)}, f32[4096]{0:T(1024)}, u32[]{:S(2)}) copy-start(f32[4096]{0:T(1024)} %param.11) | copy-start | bytes 49156
where the time goes:
time: 137 us; the launch traced here: 136 us
  other arithmetic  34.5 us (25%)
  starting transfers between devices  28.7 us (21%)
  waiting for transfers between devices  27.4 us (20%)
  blocking collectives  25.2 us (18%)
  matrix products  15.7 us (11%)
  local copies, waits for them, and re-layouts  4.13 us (3%)
    ppermute x6, waiting for transfers between devices, from_partner(): lax.ppermute(shard, axis, [(i, i ^ 1 << apart) for i in range(lax.axis_si...  27.4 us
    all_to_all x1, blocking collectives, local(): lax.all_to_all(mixed, 'heads', split_axis=0, concat_axis=1, tiled=True)  25.2 us
    ppermute x6, starting transfers between devices, from_partner(): lax.ppermute(shard, axis, [(i, i ^ 1 << apart) for i in range(lax.axis_si...  23.2 us
    eq x5, other arithmetic, local(): level_table[None] == level_id  10.8 us
    mul x2, other arithmetic, local(): row_weights = level_weights[level_id] * near_scale[level_id]  8.77 us
    dot_general x1, matrix products, local(): jnp.einsum('hqk,khd->qhd', near_weights, context_values[WINDOW:WINDOW + q...  6.39 us
    sub x1, other arithmetic, local(): exp_scores = jnp.where(in_window[None], jnp.exp(scores - row_max), 0.0)  5.72 us
    ppermute x2, starting transfers between devices, passed_along(): lax.ppermute(value, axis, [(source, source + steps) for source in range(l...  5.51 us
  transfers between devices with their start and end apart: 8, of which 5 were waited for; matrix products, arithmetic and copies ran while one was open for 32% of the time, Pallas kernels for 0%

commit v1 on v0

v1 whole, which is shorter than its diff:
```python
import functools
import math

import jax
import jax.numpy as jnp
from jax import lax
from jax.experimental import pallas as pl
from jax.experimental.pallas import tpu as pltpu
from jax.sharding import PartitionSpec as P

HEAD_DIM = 128
EPSILON = 1e-06
NEAR_LEVELS = 10
FAR_LEVELS = 6
TILE = 128
MESH = pl.DeviceIdType.MESH
F32 = jnp.float32
BF16 = jnp.bfloat16
SCALE = HEAD_DIM**-0.5
NEG = -1e30


def level_scale(level):
    return 2.0 ** (-0.5 * max(level - 1, 0))


def dot_nt(a, b):
    return lax.dot_general(a, b, (((1,), (1,)), ((), ())), preferred_element_type=F32)


def dot_nn(a, b):
    return jnp.dot(a, b, preferred_element_type=F32)


def kernel(
    rows_x,
    rows_y,
    groups,
    q_hbm,
    k_hbm,
    v_hbm,
    lw_hbm,
    gate_hbm,
    gain_ref,
    out_ref,
    q,
    k,
    v,
    vt,
    kp,
    vpt,
    lw,
    gate,
    silu,
    acc,
    mix,
    tok,
    st,
    gat,
    bsrc,
    tsrc,
    tbuf,
    xsrc,
    bk,
    q_sem,
    k_sem,
    v_sem,
    lw_sem,
    gate_sem,
    a_send,
    a_recv,
    z_send,
    z_recv,
    ks_send,
    ks_recv,
    vs_send,
    vs_recv,
    t_send,
    t_recv,
    c_send,
    c_recv,
    h_send,
    h_recv,
    o_send,
    o_recv,
):
    heads = k.shape[0]
    toks = k.shape[1]
    tiles = toks // TILE
    row_n = rows_y * 2
    seq_n = rows_x * row_n
    half = heads * HEAD_DIM // 2
    part = half // rows_y
    out_rows = toks // groups
    me = lax.axis_index("seq")
    zed = lax.axis_index("heads")
    x = me // row_n
    r = lax.rem(me, row_n)
    y = r // 2
    c = lax.rem(r, 2)

    def head_at(core, step):
        return lax.rem(core * (heads // 2) + step, heads)

    def row_id(place):
        return x * row_n + place

    loads = []
    for h in range(heads):
        cols = pl.ds(h * HEAD_DIM, HEAD_DIM)
        for src, dst, sem in ((k_hbm, k, k_sem), (v_hbm, v, v_sem), (q_hbm, q, q_sem)):
            copy = pltpu.make_async_copy(src.at[:, cols], dst.at[h], sem.at[h])
            copy.start()
            loads.append(copy)
    lw_copies = [
        pltpu.make_async_copy(lw_hbm.at[:, pl.ds(h, 1), :], lw.at[h], lw_sem.at[h])
        for h in range(heads)
    ]
    for copy in lw_copies:
        copy.start()
    gate_copy = pltpu.make_async_copy(gate_hbm, gate, gate_sem)
    gate_copy.start()

    barrier = pltpu.get_barrier_semaphore()
    after = lax.rem(me + 1, seq_n)
    before = lax.rem(me + seq_n - 1, seq_n)
    greeted = 0
    for place in (after, before):
        pl.semaphore_signal(barrier, inc=1, device_id={"seq": place}, device_id_type=MESH)
        greeted += 1
    for step in range(1, row_n):
        pl.semaphore_signal(
            barrier,
            inc=1,
            device_id={"seq": row_id(lax.rem(r + step, row_n))},
            device_id_type=MESH,
        )
        greeted += 1
    for step in range(1, rows_x):
        pl.semaphore_signal(
            barrier,
            inc=1,
            device_id={"seq": lax.rem(x + step, rows_x) * row_n + r},
            device_id_type=MESH,
        )
        greeted += 1
    for step in range(1, groups):
        pl.semaphore_signal(
            barrier,
            inc=1,
            device_id={"heads": lax.rem(zed + step, groups)},
            device_id_type=MESH,
        )
        greeted += 1

    for h in range(heads):
        pltpu.make_async_copy(k_hbm.at[:, pl.ds(0, HEAD_DIM)], k.at[h], k_sem.at[h]).wait()
        pltpu.make_async_copy(v_hbm.at[:, pl.ds(0, HEAD_DIM)], v.at[h], v_sem.at[h]).wait()
        turned = v[h].T
        vt[h] = turned
        st[pl.ds(h * HEAD_DIM, HEAD_DIM), :] = dot_nn(turned, k[h]).astype(BF16)

    pl.semaphore_wait(barrier, greeted)

    for step in range(1, row_n):
        place = lax.rem(r + step, row_n)
        rows = pl.multiple_of(lax.rem(place, 2) * half + (place // 2) * part, part)
        pltpu.make_async_remote_copy(
            st.at[pl.ds(rows, part), :],
            gat.at[r],
            a_send,
            a_recv,
            device_id={"seq": row_id(place)},
            device_id_type=MESH,
        ).start()
    mine = pl.multiple_of(c * half + y * part, part)
    gat[r] = st[pl.ds(mine, part), :]

    sibling = me + 1 - 2 * c

    @pl.when(c == 0)
    def _():
        pltpu.make_async_remote_copy(
            st, bk.at[0], z_send, z_recv, device_id={"seq": sibling}, device_id_type=MESH
        ).start()

    def send_window(step, carry):
        h = head_at(1 - c, step)
        pltpu.make_async_remote_copy(
            k.at[h],
            kp.at[h],
            ks_send.at[step],
            ks_recv.at[step],
            device_id={"seq": after},
            device_id_type=MESH,
        ).start()
        pltpu.make_async_remote_copy(
            vt.at[h],
            vpt.at[h],
            vs_send.at[step],
            vs_recv.at[step],
            device_id={"seq": after},
            device_id_type=MESH,
        ).start()
        return carry

    lax.fori_loop(0, heads, send_window, 0)

    @pl.when(c == 0)
    def _():
        bk[0] = jnp.zeros(bk.shape[1:], BF16)

    def bit_of(level):
        return lax.rem(me // (1 << level), 2)

    for level in range(1, FAR_LEVELS):

        @pl.when(bit_of(level) == 0)
        def _():
            bk[level] = jnp.zeros(bk.shape[1:], BF16)

    gate_copy.wait()
    wide = gate[...].astype(F32)
    silu[...] = wide * jax.nn.sigmoid(wide)

    pltpu.make_async_copy(
        gat.at[pl.ds(0, row_n - 1)], gat.at[pl.ds(0, row_n - 1)], a_recv
    ).wait()
    sums = [gat[i].astype(F32) for i in range(row_n)]
    level_sums = []
    while len(sums) > 1:
        sums = [sums[2 * i] + sums[2 * i + 1] for i in range(len(sums) // 2)]
        level_sums.append(sums)
    low_levels = len(level_sums) - 1
    firsts = []
    count = 0
    for level_list in level_sums[:-1]:
        firsts.append(count)
        for i in range(0, len(level_list), 2):
            bsrc[count] = level_list[i].astype(BF16)
            count += 1
    total = level_sums[-1][0]
    tsrc[...] = total
    tbuf[x] = total
    for step in range(1, rows_x):
        pltpu.make_async_remote_copy(
            tsrc,
            tbuf.at[x],
            t_send,
            t_recv,
            device_id={"seq": lax.rem(x + step, rows_x) * row_n + r},
            device_id_type=MESH,
        ).start()
    for level in range(low_levels, 0, -1):
        for step in (4, 3, 5, 2, 6, 1, 7, 0):
            place = lax.rem(y + step, rows_y)
            src = bsrc.at[firsts[level - 1] + place // (1 << level)]
            dst = bk.at[level, pl.ds(mine, part), :]

            @pl.when(lax.rem(place // (1 << (level - 1)), 2) == 1)
            def _():
                if step == 0:
                    pltpu.make_async_copy(src, dst, c_recv.at[level]).start()
                else:
                    pltpu.make_async_remote_copy(
                        src,
                        dst,
                        c_send.at[level],
                        c_recv.at[level],
                        device_id={"seq": row_id(place * 2 + c)},
                        device_id_type=MESH,
                    ).start()

    for h in range(heads):
        pltpu.make_async_copy(q_hbm.at[:, pl.ds(0, HEAD_DIM)], q.at[h], q_sem.at[h]).wait()
    for copy in lw_copies:
        copy.wait()
    key_at = lax.broadcasted_iota(jnp.int32, (TILE, TILE), 0)
    query_at = lax.broadcasted_iota(jnp.int32, (TILE, TILE), 1)
    gain_exp = SCALE * math.log2(math.e)

    def window(step, carry):
        h = head_at(c, step)
        pltpu.make_async_copy(k.at[h], kp.at[h], ks_recv.at[step]).wait()
        pltpu.make_async_copy(vt.at[h], vpt.at[h], vs_recv.at[step]).wait()
        causal = key_at <= query_at
        apart = key_at ^ query_at
        for i in range(tiles):
            cols = pl.ds(i * TILE, TILE)
            query = q[h, cols, :]
            own = dot_nt(k[h, pl.ds(0, (i + 1) * TILE), :], query)
            past = dot_nt(kp[h, pl.ds(i * TILE, toks - i * TILE), :], query)
            past = jnp.where(me == 0, NEG, past)
            own_tiles = [own[j * TILE : (j + 1) * TILE] for j in range(i + 1)]
            past_tiles = [past[j * TILE : (j + 1) * TILE] for j in range(tiles - i)]
            both = own_tiles[:-1] + [jnp.where(causal, own_tiles[-1], past_tiles[0])] + past_tiles[1:]
            top = functools.reduce(jnp.maximum, both)
            top = jnp.max(top, axis=0, keepdims=True) * gain_exp
            powers = [jnp.exp2(tile * gain_exp - top) for tile in both]
            mass = jnp.sum(functools.reduce(jnp.add, powers), axis=0, keepdims=True)
            share = 1.0 / mass
            weights = [power * share for power in powers]
            rows = [
                lw[h, level, :, cols] * (level_scale(level) * SCALE)
                for level in range(NEAR_LEVELS)
            ]
            own_weights = []
            for j in range(i):
                level = TILE.bit_length() - 1 + (i ^ j).bit_length()
                own_weights.append((weights[j] + own_tiles[j] * rows[level]).astype(BF16))
            mixed = jnp.broadcast_to(rows[0], (TILE, TILE))
            for level in range(1, TILE.bit_length()):
                mixed = jnp.where(apart >= 1 << (level - 1), rows[level], mixed)
            own_weights.append(
                jnp.where(causal, weights[i] + own_tiles[i] * mixed, 0.0).astype(BF16)
            )
            past_weights = [jnp.where(causal, 0.0, weights[i]).astype(BF16)]
            past_weights += [weight.astype(BF16) for weight in weights[i + 1 :]]
            found = dot_nn(vt[h, :, pl.ds(0, (i + 1) * TILE)], jnp.concatenate(own_weights, axis=0))
            found += dot_nn(
                vpt[h, :, pl.ds(i * TILE, toks - i * TILE)], jnp.concatenate(past_weights, axis=0)
            )
            acc[h, :, cols] = found
        return carry

    window(0, 0)

    pltpu.make_async_copy(
        tbuf.at[pl.ds(0, rows_x - 1)], tbuf.at[pl.ds(0, rows_x - 1)], t_recv
    ).wait()
    xsrc[0] = tbuf[lax.max(x - 1, 0)].astype(BF16)
    xsrc[1] = (tbuf[0] + tbuf[1]).astype(BF16)
    for up in range(FAR_LEVELS - 1 - low_levels):
        level = low_levels + 1 + up

        @pl.when(bit_of(level) == 1)
        def _():
            for step in (4, 3, 5, 2, 6, 1, 7, 0):
                place = lax.rem(y + step, rows_y)
                src = xsrc.at[up]
                dst = bk.at[level, pl.ds(mine, part), :]
                if step == 0:
                    pltpu.make_async_copy(src, dst, c_recv.at[level]).start()
                else:
                    pltpu.make_async_remote_copy(
                        src,
                        dst,
                        c_send.at[level],
                        c_recv.at[level],
                        device_id={"seq": row_id(place * 2 + c)},
                        device_id_type=MESH,
                    ).start()

    lax.fori_loop(1, heads, window, 0)

    my_half = pl.ds(pl.multiple_of(c * half, half), half)
    other_half = pl.ds(pl.multiple_of((1 - c) * half, half), half)
    for level in range(1, FAR_LEVELS):

        @pl.when(bit_of(level) == 1)
        def _():
            piece = bk.at[level, my_half, :]
            pltpu.make_async_copy(piece, piece, c_recv.at[level]).wait()
            pltpu.make_async_remote_copy(
                piece,
                piece,
                h_send.at[level],
                h_recv.at[level],
                device_id={"seq": sibling},
                device_id_type=MESH,
            ).start()

    @pl.when(c == 1)
    def _():
        pltpu.make_async_copy(st, bk.at[0], z_recv).wait()

    wide_cols = min(2 * TILE, toks)

    def far(step, carry):
        h = head_at(c, step)

        @pl.when(step == heads // 2)
        def _():
            for level in range(1, FAR_LEVELS):

                @pl.when(bit_of(level) == 1)
                def _():
                    piece = bk.at[level, other_half, :]
                    pltpu.make_async_copy(piece, piece, h_recv.at[level]).wait()

        rows = pl.ds(pl.multiple_of(h * HEAD_DIM, HEAD_DIM), HEAD_DIM)
        for start in range(0, toks, wide_cols):
            cols = pl.ds(start, wide_cols)
            query = q[h, cols, :]
            found = acc[h, :, cols]
            for level in range(FAR_LEVELS):
                weight = lw[h, NEAR_LEVELS + level, :, cols]
                weight = weight * (level_scale(NEAR_LEVELS + level) * SCALE)
                found += dot_nt(bk[level, rows, :], query) * weight
            mix[h, cols, :] = found.T.astype(BF16)
        for hop in (4, 3, 5, 2, 6, 1, 7):
            there = lax.rem(zed + hop, groups)
            pltpu.make_async_remote_copy(
                mix.at[h, pl.ds(pl.multiple_of(there * out_rows, out_rows), out_rows), :],
                tok.at[zed * heads + h],
                o_send.at[step],
                o_recv.at[step],
                device_id={"heads": there},
                device_id_type=MESH,
            ).start()
        tok[zed * heads + h] = mix[h, pl.ds(pl.multiple_of(zed * out_rows, out_rows), out_rows), :]
        return carry

    lax.fori_loop(0, heads, far, 0)

    lanes = jnp.zeros((out_rows, HEAD_DIM), F32)
    for step in range(heads):
        piece = tok.at[pl.ds(0, groups - 1)]
        pltpu.make_async_copy(piece, piece, o_recv.at[step]).wait()
        h = head_at(c, step)
        for group in range(groups):
            index = group * heads + h
            cols = pl.ds(pl.multiple_of(index * HEAD_DIM, HEAD_DIM), HEAD_DIM)
            gated = tok[index].astype(F32) * silu[:, cols]
            silu[:, cols] = gated
            lanes += gated * gated
    square = jnp.sum(lanes, axis=1, keepdims=True) * (1.0 / (groups * heads * HEAD_DIM))
    inverse = lax.rsqrt(square + EPSILON)
    for index in range(groups * heads):
        cols = pl.ds(index * HEAD_DIM, HEAD_DIM)
        out_ref[:, cols] = (gain_ref[:, cols] * silu[:, cols] * inverse).astype(BF16)

    piece = gat.at[pl.ds(0, row_n - 1)]
    pltpu.make_async_copy(piece, piece, a_send).wait()

    @pl.when(c == 0)
    def _():
        pltpu.make_async_copy(st, st, z_send).wait()

    for step in range(heads):
        pltpu.make_async_copy(k.at[0], k.at[0], ks_send.at[step]).wait()
        pltpu.make_async_copy(vt.at[0], vt.at[0], vs_send.at[step]).wait()
        piece = tok.at[pl.ds(0, groups - 1)]
        pltpu.make_async_copy(piece, piece, o_send.at[step]).wait()
    piece = tbuf.at[pl.ds(0, rows_x - 1)]
    pltpu.make_async_copy(piece, piece, t_send).wait()
    for level in range(1, FAR_LEVELS):
        if level <= low_levels:
            for own_bit in range(2):

                @pl.when(bit_of(level) == own_bit)
                def _():
                    piece = gat.at[pl.ds(0, rows_y // 2 - own_bit)]
                    pltpu.make_async_copy(piece, piece, c_send.at[level]).wait()

        else:

            @pl.when(bit_of(level) == 1)
            def _():
                piece = gat.at[pl.ds(0, rows_y - 1)]
                pltpu.make_async_copy(piece, piece, c_send.at[level]).wait()

        @pl.when(bit_of(level) == 1)
        def _():
            piece = bk.at[level, my_half, :]
            pltpu.make_async_copy(piece, piece, h_send.at[level]).wait()


def local(rows_x, rows_y, queries, key_vectors, values, level_weights, gate_branch, norm_gain):
    toks, width = queries.shape
    heads = width // HEAD_DIM
    groups = lax.axis_size("heads")
    out_rows, model = gate_branch.shape
    row_n = rows_y * 2
    part = heads * HEAD_DIM // row_n
    dma = pltpu.SemaphoreType.DMA
    hbm = pl.BlockSpec(memory_space=pl.ANY)
    vmem = pl.BlockSpec(memory_space=pltpu.VMEM)
    head_shape = (heads, toks, HEAD_DIM)
    turned_shape = (heads, HEAD_DIM, toks)
    return pl.pallas_call(
        functools.partial(kernel, rows_x, rows_y, groups),
        out_shape=jax.ShapeDtypeStruct((out_rows, model), BF16),
        in_specs=[hbm] * 5 + [vmem],
        out_specs=vmem,
        scratch_shapes=[
            pltpu.VMEM(head_shape, BF16),
            pltpu.VMEM(head_shape, BF16),
            pltpu.VMEM(head_shape, BF16),
            pltpu.VMEM(turned_shape, BF16),
            pltpu.VMEM(head_shape, BF16),
            pltpu.VMEM(turned_shape, BF16),
            pltpu.VMEM((heads, level_weights.shape[0], 1, toks), F32),
            pltpu.VMEM(gate_branch.shape, BF16),
            pltpu.VMEM(gate_branch.shape, F32),
            pltpu.VMEM(turned_shape, F32),
            pltpu.VMEM(head_shape, BF16),
            pltpu.VMEM((groups * heads, out_rows, HEAD_DIM), BF16),
            pltpu.VMEM((heads * HEAD_DIM, HEAD_DIM), BF16),
            pltpu.VMEM((row_n, part, HEAD_DIM), BF16),
            pltpu.VMEM((row_n // 2 - 1, part, HEAD_DIM), BF16),
            pltpu.VMEM((part, HEAD_DIM), F32),
            pltpu.VMEM((rows_x, part, HEAD_DIM), F32),
            pltpu.VMEM((2, part, HEAD_DIM), BF16),
            pltpu.VMEM((FAR_LEVELS, heads * HEAD_DIM, HEAD_DIM), BF16),
            dma((heads,)),
            dma((heads,)),
            dma((heads,)),
            dma((heads,)),
            dma,
            dma,
            dma,
            dma,
            dma,
            dma((heads,)),
            dma((heads,)),
            dma((heads,)),
            dma((heads,)),
            dma,
            dma,
            dma((FAR_LEVELS,)),
            dma((FAR_LEVELS,)),
            dma((FAR_LEVELS,)),
            dma((FAR_LEVELS,)),
            dma((heads,)),
            dma((heads,)),
        ],
        compiler_params=pltpu.CompilerParams(
            collective_id=0, has_side_effects=True, vmem_limit_bytes=40 << 20
        ),
        name="layer",
    )(queries, key_vectors, values, level_weights, gate_branch, norm_gain.reshape(1, -1))


def solution(mesh):
    rows_x, rows_y = 4, 8
    return jax.shard_map(
        functools.partial(local, rows_x, rows_y),
        mesh=mesh,
        in_specs=(
            P("seq", "heads"),
            P("seq", "heads"),
            P("seq", "heads"),
            P(None, "heads", "seq"),
            P(("seq", "heads"), None),
            P(),
        ),
        out_specs=P(("seq", "heads"), None),
        check_vma=False,
    )
```

time: 137 us -> 57.7 us (0.42)
  the two profiles are of different devices: /device:TPU:6 before, /device:TPU:4 now
where the time goes in v1:
time: 57.7 us; the launch traced here: 57.4 us
  Pallas kernels  50.8 us (88%)
  local copies, waits for them, and re-layouts  6.58 us (11%)
    pallas_call x1, Pallas kernels, local(): pl.pallas_call(functools.partial(kernel, rows_x, rows_y, groups), out_sha...  50.8 us
    unnamed x13, local copies, waits for them, and re-layouts  6.58 us

profile of v1, /device:TPU:4, one launch (start us, length us, event | category | flops | bytes accessed | tf_op | source)
XLA Modules:
  0.0 57.4 jit_solution(15170487819887024277)
XLA Ops:
  0.0 0.0 copy-start
  0.0 1.0 %copy-done = bf16[512,512]{1,0:T(8,128)(2,1)S(1)} copy-done((bf16[512,512]{1,0:T(8,128)(2,1)S(1)}, bf16[512,512]{1,0:T(8,128)(2,1)}, u32[]{:S(2)}) %copy-start) | copy-done | bytes 524312
  1.0 0.0 copy-start.1
  1.0 1.0 %copy-done.1 = bf16[512,512]{1,0:T(8,128)(2,1)S(1)} copy-done((bf16[512,512]{1,0:T(8,128)(2,1)S(1)}, bf16[512,512]{1,0:T(8,128)(2,1)}, u32[]{:S(2)}) %copy-start.1) | copy-done | bytes 524312
  2.1 0.0 copy-start.2
  2.1 1.0 %copy-done.2 = bf16[512,512]{1,0:T(8,128)(2,1)S(1)} copy-done((bf16[512,512]{1,0:T(8,128)(2,1)S(1)}, bf16[512,512]{1,0:T(8,128)(2,1)}, u32[]{:S(2)}) %copy-start.2) | copy-done | bytes 524312
  3.1 0.0 copy-start.3
  3.1 1.0 %copy-done.3 = bf16[64,4096]{1,0:T(8,128)(2,1)S(1)} copy-done((bf16[64,4096]{1,0:T(8,128)(2,1)S(1)}, bf16[64,4096]{1,0:T(8,128)(2,1)}, u32[]{:S(2)}) %copy-start.3) | copy-done | bytes 524312
  4.2 0.0 copy-start.4
  4.2 0.9 %copy-done.4 = f32[16,4,512]{2,1,0:T(4,128)S(1)} copy-done((f32[16,4,512]{2,1,0:T(4,128)S(1)}, f32[16,4,512]{2,1,0:T(4,128)}, u32[]{:S(2)}) %copy-start.4) | copy-done | bytes 131096
  5.1 0.0 copy-start.5
  5.1 0.7 %copy-done.5 = f32[4096]{0:T(1024)S(1)} copy-done((f32[4096]{0:T(1024)S(1)}, f32[4096]{0:T(1024)}, u32[]{:S(2)}) %copy-start.5) | copy-done | bytes 16408
  5.8 50.8 %layer.1 = bf16[64,4096]{1,0:T(8,128)(2,1)S(1)} custom-call(bf16[512,512]{1,0:T(8,128)(2,1)S(1)} %copy-done, bf16[512,512]{1,0:T(8,128)(2,1)S(1)} %copy-done.1, bf16[512,512]{1,0:T(8,128)(2,1)S(1)} %copy-done.2, f32[16,4,512]{2,1,0:T(4,128)S(1)} %copy-done.4, bf16[64,4096]{1,0:T(8,128)(2,1)S(1)} %copy-done.3, f32[1,4096]{1,0:T(1,128)S(1)} %bitcast.1), custom_call_target="tpu_custom_call" | custom-call | tf_op jit(solution)/shard_map/layer/pallas_call | solution.py:481
  56.6 0.8 %copy.8 = bf16[64,4096]{1,0:T(8,128)(2,1)} copy(bf16[64,4096]{1,0:T(8,128)(2,1)S(1)} %layer.1) | data formatting | bytes 1048576
Async XLA Ops:
  0.0 1.0 %copy-start = (bf16[512,512]{1,0:T(8,128)(2,1)S(1)}, bf16[512,512]{1,0:T(8,128)(2,1)}, u32[]{:S(2)}) copy-start(bf16[512,512]{1,0:T(8,128)(2,1)} %q_hbm.1) | copy-start | bytes 1572868
  1.0 1.0 %copy-start.1 = (bf16[512,512]{1,0:T(8,128)(2,1)S(1)}, bf16[512,512]{1,0:T(8,128)(2,1)}, u32[]{:S(2)}) copy-start(bf16[512,512]{1,0:T(8,128)(2,1)} %k_hbm.1) | copy-start | bytes 1572868
  2.1 1.0 %copy-start.2 = (bf16[512,512]{1,0:T(8,128)(2,1)S(1)}, bf16[512,512]{1,0:T(8,128)(2,1)}, u32[]{:S(2)}) copy-start(bf16[512,512]{1,0:T(8,128)(2,1)} %v_hbm.1) | copy-start | bytes 1572868
  3.1 1.0 %copy-start.3 = (bf16[64,4096]{1,0:T(8,128)(2,1)S(1)}, bf16[64,4096]{1,0:T(8,128)(2,1)}, u32[]{:S(2)}) copy-start(bf16[64,4096]{1,0:T(8,128)(2,1)} %gate_hbm.1) | copy-start | bytes 1572868
  4.2 0.9 %copy-start.4 = (f32[16,4,512]{2,1,0:T(4,128)S(1)}, f32[16,4,512]{2,1,0:T(4,128)}, u32[]{:S(2)}) copy-start(f32[16,4,512]{2,1,0:T(4,128)} %lw_hbm.1) | copy-start | bytes 393220
  5.1 0.7 %copy-start.5 = (f32[4096]{0:T(1024)S(1)}, f32[4096]{0:T(1024)}, u32[]{:S(2)}) copy-start(f32[4096]{0:T(1024)} %param.11) | copy-start | bytes 49156

commit v2 on v1

--- a/solution.py
+++ b/solution.py
@@ -41,7 +41,7 @@
     v_hbm,
     lw_hbm,
     gate_hbm,
-    gain_ref,
+    gain_hbm,
     out_ref,
     q,
     k,
@@ -62,11 +62,13 @@
     tbuf,
     xsrc,
     bk,
+    gain_ref,
     q_sem,
     k_sem,
     v_sem,
     lw_sem,
     gate_sem,
+    gain_sem,
     a_send,
     a_recv,
     z_send,
@@ -83,6 +85,7 @@
     h_recv,
     o_send,
     o_recv,
+    here_sem,
 ):
     heads = k.shape[0]
     toks = k.shape[1]
@@ -104,22 +107,6 @@
 
     def row_id(place):
         return x * row_n + place
-
-    loads = []
-    for h in range(heads):
-        cols = pl.ds(h * HEAD_DIM, HEAD_DIM)
-        for src, dst, sem in ((k_hbm, k, k_sem), (v_hbm, v, v_sem), (q_hbm, q, q_sem)):
-            copy = pltpu.make_async_copy(src.at[:, cols], dst.at[h], sem.at[h])
-            copy.start()
-            loads.append(copy)
-    lw_copies = [
-        pltpu.make_async_copy(lw_hbm.at[:, pl.ds(h, 1), :], lw.at[h], lw_sem.at[h])
-        for h in range(heads)
-    ]
-    for copy in lw_copies:
-        copy.start()
-    gate_copy = pltpu.make_async_copy(gate_hbm, gate, gate_sem)
-    gate_copy.start()
 
     barrier = pltpu.get_barrier_semaphore()
     after = lax.rem(me + 1, seq_n)
@@ -145,13 +132,31 @@
         )
         greeted += 1
     for step in range(1, groups):
-        pl.semaphore_signal(
-            barrier,
-            inc=1,
-            device_id={"heads": lax.rem(zed + step, groups)},
-            device_id_type=MESH,
-        )
-        greeted += 1
+
+        @pl.when(zed + step < groups)
+        def _():
+            pl.semaphore_signal(
+                barrier, inc=1, device_id={"heads": zed + step}, device_id_type=MESH
+            )
+
+
+    loads = []
+    for h in range(heads):
+        cols = pl.ds(h * HEAD_DIM, HEAD_DIM)
+        for src, dst, sem in ((k_hbm, k, k_sem), (v_hbm, v, v_sem), (q_hbm, q, q_sem)):
+            copy = pltpu.make_async_copy(src.at[:, cols], dst.at[h], sem.at[h])
+            copy.start()
+            loads.append(copy)
+    lw_copies = [
+        pltpu.make_async_copy(lw_hbm.at[:, pl.ds(h, 1), :], lw.at[h], lw_sem.at[h])
+        for h in range(heads)
+    ]
+    for copy in lw_copies:
+        copy.start()
+    gate_copy = pltpu.make_async_copy(gate_hbm, gate, gate_sem)
+    gate_copy.start()
+    gain_copy = pltpu.make_async_copy(gain_hbm, gain_ref, gain_sem)
+    gain_copy.start()
 
     for h in range(heads):
         pltpu.make_async_copy(k_hbm.at[:, pl.ds(0, HEAD_DIM)], k.at[h], k_sem.at[h]).wait()
@@ -160,7 +165,15 @@
         vt[h] = turned
         st[pl.ds(h * HEAD_DIM, HEAD_DIM), :] = dot_nn(turned, k[h]).astype(BF16)
 
-    pl.semaphore_wait(barrier, greeted)
+    pl.semaphore_wait(barrier, greeted + zed)
+    for step in range(1, groups):
+
+        @pl.when(zed >= step)
+        def _():
+            pl.semaphore_signal(
+                here_sem, inc=1, device_id={"heads": zed - step}, device_id_type=MESH
+            )
+
 
     for step in range(1, row_n):
         place = lax.rem(r + step, row_n)
@@ -184,7 +197,7 @@
             st, bk.at[0], z_send, z_recv, device_id={"seq": sibling}, device_id_type=MESH
         ).start()
 
-    def send_window(step, carry):
+    def send_window(step):
         h = head_at(1 - c, step)
         pltpu.make_async_remote_copy(
             k.at[h],
@@ -202,9 +215,8 @@
             device_id={"seq": after},
             device_id_type=MESH,
         ).start()
-        return carry
-
-    lax.fori_loop(0, heads, send_window, 0)
+
+    send_window(0)
 
     @pl.when(c == 0)
     def _():
@@ -220,6 +232,7 @@
             bk[level] = jnp.zeros(bk.shape[1:], BF16)
 
     gate_copy.wait()
+    gain_copy.wait()
     wide = gate[...].astype(F32)
     silu[...] = wide * jax.nn.sigmoid(wide)
 
@@ -271,6 +284,8 @@
                         device_id_type=MESH,
                     ).start()
 
+    send_window(1)
+
     for h in range(heads):
         pltpu.make_async_copy(q_hbm.at[:, pl.ds(0, HEAD_DIM)], q.at[h], q_sem.at[h]).wait()
     for copy in lw_copies:
@@ -279,7 +294,7 @@
     query_at = lax.broadcasted_iota(jnp.int32, (TILE, TILE), 1)
     gain_exp = SCALE * math.log2(math.e)
 
-    def window(step, carry):
+    def window(step):
         h = head_at(c, step)
         pltpu.make_async_copy(k.at[h], kp.at[h], ks_recv.at[step]).wait()
         pltpu.make_async_copy(vt.at[h], vpt.at[h], vs_recv.at[step]).wait()
@@ -321,9 +336,8 @@
                 vpt[h, :, pl.ds(i * TILE, toks - i * TILE)], jnp.concatenate(past_weights, axis=0)
             )
             acc[h, :, cols] = found
-        return carry
-
-    window(0, 0)
+
+    window(0)
 
     pltpu.make_async_copy(
         tbuf.at[pl.ds(0, rows_x - 1)], tbuf.at[pl.ds(0, rows_x - 1)], t_recv
@@ -351,7 +365,9 @@
                         device_id_type=MESH,
                     ).start()
 
-    lax.fori_loop(1, heads, window, 0)
+    for step in range(2, heads):
+        send_window(step)
+    window(1)
 
     my_half = pl.ds(pl.multiple_of(c * half, half), half)
     other_half = pl.ds(pl.multiple_of((1 - c) * half, half), half)
@@ -376,17 +392,8 @@
 
     wide_cols = min(2 * TILE, toks)
 
-    def far(step, carry):
+    def far(step):
         h = head_at(c, step)
-
-        @pl.when(step == heads // 2)
-        def _():
-            for level in range(1, FAR_LEVELS):
-
-                @pl.when(bit_of(level) == 1)
-                def _():
-                    piece = bk.at[level, other_half, :]
-                    pltpu.make_async_copy(piece, piece, h_recv.at[level]).wait()
 
         rows = pl.ds(pl.multiple_of(h * HEAD_DIM, HEAD_DIM), HEAD_DIM)
         for start in range(0, toks, wide_cols):
@@ -409,9 +416,33 @@
                 device_id_type=MESH,
             ).start()
         tok[zed * heads + h] = mix[h, pl.ds(pl.multiple_of(zed * out_rows, out_rows), out_rows), :]
+
+    @pl.when(zed < groups - 1)
+    def _():
+        pl.semaphore_wait(here_sem, groups - 1 - zed)
+
+    def first(step, carry):
+        far(step)
         return carry
 
-    lax.fori_loop(0, heads, far, 0)
+    lax.fori_loop(0, heads // 2, first, 0)
+
+    def second(step, carry):
+        window(step)
+
+        @pl.when(step == heads // 2)
+        def _():
+            for level in range(1, FAR_LEVELS):
+
+                @pl.when(bit_of(level) == 1)
+                def _():
+                    piece = bk.at[level, other_half, :]
+                    pltpu.make_async_copy(piece, piece, h_recv.at[level]).wait()
+
+        far(step)
+        return carry
+
+    lax.fori_loop(heads // 2, heads, second, 0)
 
     lanes = jnp.zeros((out_rows, HEAD_DIM), F32)
     for step in range(heads):
@@ -481,7 +512,7 @@
     return pl.pallas_call(
         functools.partial(kernel, rows_x, rows_y, groups),
         out_shape=jax.ShapeDtypeStruct((out_rows, model), BF16),
-        in_specs=[hbm] * 5 + [vmem],
+        in_specs=[hbm] * 6,
         out_specs=vmem,
         scratch_shapes=[
             pltpu.VMEM(head_shape, BF16),
@@ -503,10 +534,12 @@
             pltpu.VMEM((rows_x, part, HEAD_DIM), F32),
             pltpu.VMEM((2, part, HEAD_DIM), BF16),
             pltpu.VMEM((FAR_LEVELS, heads * HEAD_DIM, HEAD_DIM), BF16),
-            dma((heads,)),
-            dma((heads,)),
-            dma((heads,)),
-            dma((heads,)),
+            pltpu.VMEM((1, model), F32),
+            dma((heads,)),
+            dma((heads,)),
+            dma((heads,)),
+            dma((heads,)),
+            dma,
             dma,
             dma,
             dma,
@@ -524,9 +557,10 @@
             dma((FAR_LEVELS,)),
             dma((heads,)),
             dma((heads,)),
+            pltpu.SemaphoreType.REGULAR,
         ],
         compiler_params=pltpu.CompilerParams(
-            collective_id=0, has_side_effects=True, vmem_limit_bytes=40 << 20
+            collective_id=0, has_side_effects=True, vmem_limit_bytes=67043328
         ),
         name="layer",
     )(queries, key_vectors, values, level_weights, gate_branch, norm_gain.reshape(1, -1))

time: 57.7 us -> 48.4 us (0.84)
  the two profiles are of different devices: /device:TPU:4 before, /device:TPU:3 now
where the time goes in v2:
time: 48.4 us; the launch traced here: 48.3 us
  Pallas kernels  46.4 us (96%)
  local copies, waits for them, and re-layouts  1.87 us (4%)
    pallas_call x1, Pallas kernels, local(): pl.pallas_call(functools.partial(kernel, rows_x, rows_y, groups), out_sha...  46.4 us
    unnamed x1, local copies, waits for them, and re-layouts  1.87 us

profile of v2, /device:TPU:3, one launch (start us, length us, event | category | flops | bytes accessed | tf_op | source)
XLA Modules:
  0.0 48.3 jit_solution(7910921149312447103)
XLA Ops:
  0.0 46.4 %layer.1 = bf16[64,4096]{1,0:T(8,128)(2,1)} custom-call(bf16[512,512]{1,0:T(8,128)(2,1)} %q_hbm.1, bf16[512,512]{1,0:T(8,128)(2,1)} %k_hbm.1, bf16[512,512]{1,0:T(8,128)(2,1)} %v_hbm.1, f32[16,4,512]{2,1,0:T(4,128)} %lw_hbm.1, bf16[64,4096]{1,0:T(8,128)(2,1)} %gate_hbm.1, f32[1,4096]{1,0:T(1,128)} %bitcast.1), custom_call_target="tpu_custom_call" | custom-call | tf_op jit(solution)/shard_map/layer/pallas_call | solution.py:512
  46.4 1.9 %copy.8 = bf16[64,4096]{1,0:T(8,128)(2,1)} copy(bf16[64,4096]{1,0:T(8,128)(2,1)} %layer.1) | data formatting | bytes 1048576

commit v3 on v2

--- a/solution.py
+++ b/solution.py
@@ -47,8 +47,13 @@
     k,
     v,
     vt,
-    kp,
-    vpt,
+    qn,
+    past_out,
+    past_in,
+    stat_out,
+    stat_in,
+    own_acc,
+    own_stat,
     lw,
     gate,
     silu,
@@ -73,10 +78,12 @@
     a_recv,
     z_send,
     z_recv,
-    ks_send,
-    ks_recv,
-    vs_send,
-    vs_recv,
+    qs_send,
+    qs_recv,
+    ps_send,
+    ps_recv,
+    ss_send,
+    ss_recv,
     t_send,
     t_recv,
     c_send,
@@ -109,12 +116,15 @@
         return x * row_n + place
 
     barrier = pltpu.get_barrier_semaphore()
-    after = lax.rem(me + 1, seq_n)
-    before = lax.rem(me + seq_n - 1, seq_n)
-    greeted = 0
-    for place in (after, before):
-        pl.semaphore_signal(barrier, inc=1, device_id={"seq": place}, device_id_type=MESH)
-        greeted += 1
+    greeted = (me > 0).astype(jnp.int32) + (me < seq_n - 1).astype(jnp.int32)
+    for apart in (-1, 1):
+
+        @pl.when((me + apart >= 0) & (me + apart < seq_n))
+        def _():
+            pl.semaphore_signal(
+                barrier, inc=1, device_id={"seq": me + apart}, device_id_type=MESH
+            )
+
     for step in range(1, row_n):
         pl.semaphore_signal(
             barrier,
@@ -140,13 +150,13 @@
             )
 
 
-    loads = []
     for h in range(heads):
         cols = pl.ds(h * HEAD_DIM, HEAD_DIM)
-        for src, dst, sem in ((k_hbm, k, k_sem), (v_hbm, v, v_sem), (q_hbm, q, q_sem)):
-            copy = pltpu.make_async_copy(src.at[:, cols], dst.at[h], sem.at[h])
-            copy.start()
-            loads.append(copy)
+        pltpu.make_async_copy(v_hbm.at[:, cols], v.at[h], v_sem.at[h]).start()
+        pltpu.make_async_copy(k_hbm.at[:, cols], k.at[h], k_sem.at[h]).start()
+    for h in range(heads):
+        cols = pl.ds(h * HEAD_DIM, HEAD_DIM)
+        pltpu.make_async_copy(q_hbm.at[:, cols], q.at[h], q_sem.at[h]).start()
     lw_copies = [
         pltpu.make_async_copy(lw_hbm.at[:, pl.ds(h, 1), :], lw.at[h], lw_sem.at[h])
         for h in range(heads)
@@ -175,7 +185,7 @@
             )
 
 
-    for step in range(1, row_n):
+    for step in sorted(range(1, row_n), key=lambda step: abs(step - row_n // 2)):
         place = lax.rem(r + step, row_n)
         rows = pl.multiple_of(lax.rem(place, 2) * half + (place // 2) * part, part)
         pltpu.make_async_remote_copy(
@@ -197,26 +207,29 @@
             st, bk.at[0], z_send, z_recv, device_id={"seq": sibling}, device_id_type=MESH
         ).start()
 
-    def send_window(step):
-        h = head_at(1 - c, step)
-        pltpu.make_async_remote_copy(
-            k.at[h],
-            kp.at[h],
-            ks_send.at[step],
-            ks_recv.at[step],
-            device_id={"seq": after},
-            device_id_type=MESH,
-        ).start()
-        pltpu.make_async_remote_copy(
-            vt.at[h],
-            vpt.at[h],
-            vs_send.at[step],
-            vs_recv.at[step],
-            device_id={"seq": after},
-            device_id_type=MESH,
-        ).start()
-
-    send_window(0)
+    def send_queries(step):
+        h = head_at(c, step)
+
+        @pl.when(me > 0)
+        def _():
+            pltpu.make_async_remote_copy(
+                q.at[h],
+                qn.at[h],
+                qs_send.at[step],
+                qs_recv.at[step],
+                device_id={"seq": me - 1},
+                device_id_type=MESH,
+            ).start()
+
+    for h in range(heads):
+        pltpu.make_async_copy(q_hbm.at[:, pl.ds(0, HEAD_DIM)], q.at[h], q_sem.at[h]).wait()
+    for step in range(heads - 1):
+        send_queries(step)
+
+    @pl.when(me == 0)
+    def _():
+        past_in[...] = jnp.zeros(past_in.shape, BF16)
+        stat_in[...] = jnp.full(stat_in.shape, NEG, F32)
 
     @pl.when(c == 0)
     def _():
@@ -235,6 +248,51 @@
     gain_copy.wait()
     wide = gate[...].astype(F32)
     silu[...] = wide * jax.nn.sigmoid(wide)
+
+    for copy in lw_copies:
+        copy.wait()
+    key_at = lax.broadcasted_iota(jnp.int32, (TILE, TILE), 0)
+    query_at = lax.broadcasted_iota(jnp.int32, (TILE, TILE), 1)
+    gain_exp = SCALE * math.log2(math.e)
+
+    def within(step, carry):
+        h = head_at(c, step)
+        causal = key_at <= query_at
+        apart = key_at ^ query_at
+        for i in range(tiles):
+            cols = pl.ds(i * TILE, TILE)
+            scores = dot_nt(k[h, pl.ds(0, (i + 1) * TILE), :], q[h, cols, :])
+            parts = [scores[j * TILE : (j + 1) * TILE] for j in range(i + 1)]
+            seen = parts[:-1] + [jnp.where(causal, parts[-1], NEG)]
+            top = functools.reduce(jnp.maximum, seen)
+            top = jnp.max(top, axis=0, keepdims=True) * gain_exp
+            powers = [jnp.exp2(tile * gain_exp - top) for tile in seen]
+            mass = jnp.sum(functools.reduce(jnp.add, powers), axis=0, keepdims=True)
+            rows = [
+                lw[h, level, :, cols] * (level_scale(level) * SCALE) for level in range(NEAR_LEVELS)
+            ]
+            near = [
+                parts[j] * rows[TILE.bit_length() - 1 + (i ^ j).bit_length()] for j in range(i)
+            ]
+            mixed = jnp.broadcast_to(rows[0], (TILE, TILE))
+            for level in range(1, TILE.bit_length()):
+                mixed = jnp.where(apart >= 1 << (level - 1), rows[level], mixed)
+            near.append(jnp.where(causal, parts[i] * mixed, 0.0))
+            both = jnp.concatenate(
+                [
+                    jnp.concatenate([tile.astype(BF16) for tile in powers], axis=0),
+                    jnp.concatenate([tile.astype(BF16) for tile in near], axis=0),
+                ],
+                axis=1,
+            )
+            found = dot_nn(vt[h, :, pl.ds(0, (i + 1) * TILE)], both)
+            own_acc[h, :, cols] = found[:, :TILE]
+            acc[h, :, cols] = found[:, TILE:]
+            own_stat[h, 0:1, cols] = top
+            own_stat[h, 1:2, cols] = mass
+        return carry
+
+    lax.fori_loop(0, heads, within, 0)
 
     pltpu.make_async_copy(
         gat.at[pl.ds(0, row_n - 1)], gat.at[pl.ds(0, row_n - 1)], a_recv
@@ -284,60 +342,41 @@
                         device_id_type=MESH,
                     ).start()
 
-    send_window(1)
-
-    for h in range(heads):
-        pltpu.make_async_copy(q_hbm.at[:, pl.ds(0, HEAD_DIM)], q.at[h], q_sem.at[h]).wait()
-    for copy in lw_copies:
-        copy.wait()
-    key_at = lax.broadcasted_iota(jnp.int32, (TILE, TILE), 0)
-    query_at = lax.broadcasted_iota(jnp.int32, (TILE, TILE), 1)
-    gain_exp = SCALE * math.log2(math.e)
-
-    def window(step):
-        h = head_at(c, step)
-        pltpu.make_async_copy(k.at[h], kp.at[h], ks_recv.at[step]).wait()
-        pltpu.make_async_copy(vt.at[h], vpt.at[h], vs_recv.at[step]).wait()
-        causal = key_at <= query_at
-        apart = key_at ^ query_at
+    send_queries(heads - 1)
+
+    def onward(step, carry):
+        h = head_at(1 - c, step)
+        pltpu.make_async_copy(q.at[h], qn.at[h], qs_recv.at[step]).wait()
+        later = key_at > query_at
         for i in range(tiles):
             cols = pl.ds(i * TILE, TILE)
-            query = q[h, cols, :]
-            own = dot_nt(k[h, pl.ds(0, (i + 1) * TILE), :], query)
-            past = dot_nt(kp[h, pl.ds(i * TILE, toks - i * TILE), :], query)
-            past = jnp.where(me == 0, NEG, past)
-            own_tiles = [own[j * TILE : (j + 1) * TILE] for j in range(i + 1)]
-            past_tiles = [past[j * TILE : (j + 1) * TILE] for j in range(tiles - i)]
-            both = own_tiles[:-1] + [jnp.where(causal, own_tiles[-1], past_tiles[0])] + past_tiles[1:]
-            top = functools.reduce(jnp.maximum, both)
+            count = tiles - i
+            scores = dot_nt(k[h, pl.ds(i * TILE, count * TILE), :], qn[h, cols, :])
+            parts = [scores[j * TILE : (j + 1) * TILE] for j in range(count)]
+            seen = [jnp.where(later, parts[0], NEG)] + parts[1:]
+            top = functools.reduce(jnp.maximum, seen)
             top = jnp.max(top, axis=0, keepdims=True) * gain_exp
-            powers = [jnp.exp2(tile * gain_exp - top) for tile in both]
+            powers = [jnp.exp2(tile * gain_exp - top) for tile in seen]
+            powers[0] = jnp.where(later, powers[0], 0.0)
             mass = jnp.sum(functools.reduce(jnp.add, powers), axis=0, keepdims=True)
-            share = 1.0 / mass
-            weights = [power * share for power in powers]
-            rows = [
-                lw[h, level, :, cols] * (level_scale(level) * SCALE)
-                for level in range(NEAR_LEVELS)
-            ]
-            own_weights = []
-            for j in range(i):
-                level = TILE.bit_length() - 1 + (i ^ j).bit_length()
-                own_weights.append((weights[j] + own_tiles[j] * rows[level]).astype(BF16))
-            mixed = jnp.broadcast_to(rows[0], (TILE, TILE))
-            for level in range(1, TILE.bit_length()):
-                mixed = jnp.where(apart >= 1 << (level - 1), rows[level], mixed)
-            own_weights.append(
-                jnp.where(causal, weights[i] + own_tiles[i] * mixed, 0.0).astype(BF16)
-            )
-            past_weights = [jnp.where(causal, 0.0, weights[i]).astype(BF16)]
-            past_weights += [weight.astype(BF16) for weight in weights[i + 1 :]]
-            found = dot_nn(vt[h, :, pl.ds(0, (i + 1) * TILE)], jnp.concatenate(own_weights, axis=0))
-            found += dot_nn(
-                vpt[h, :, pl.ds(i * TILE, toks - i * TILE)], jnp.concatenate(past_weights, axis=0)
-            )
-            acc[h, :, cols] = found
-
-    window(0)
+            both = jnp.concatenate([tile.astype(BF16) for tile in powers], axis=0)
+            found = dot_nn(vt[h, :, pl.ds(i * TILE, count * TILE)], both)
+            past_out[h, :, cols] = found.astype(BF16)
+            stat_out[h, 0:1, cols] = top
+            stat_out[h, 1:2, cols] = mass
+        for src, dst, send, recv in (
+            (past_out, past_in, ps_send, ps_recv),
+            (stat_out, stat_in, ss_send, ss_recv),
+        ):
+            pltpu.make_async_remote_copy(
+                src.at[h],
+                dst.at[h],
+                send.at[step],
+                recv.at[step],
+                device_id={"seq": me + 1},
+                device_id_type=MESH,
+            ).start()
+        return carry
 
     pltpu.make_async_copy(
         tbuf.at[pl.ds(0, rows_x - 1)], tbuf.at[pl.ds(0, rows_x - 1)], t_recv
@@ -365,14 +404,15 @@
                         device_id_type=MESH,
                     ).start()
 
-    for step in range(2, heads):
-        send_window(step)
-    window(1)
+    @pl.when(me < seq_n - 1)
+    def _():
+        lax.fori_loop(0, heads, onward, 0)
+
 
     my_half = pl.ds(pl.multiple_of(c * half, half), half)
     other_half = pl.ds(pl.multiple_of((1 - c) * half, half), half)
-    for level in range(1, FAR_LEVELS):
-
+
+    def take(level):
         @pl.when(bit_of(level) == 1)
         def _():
             piece = bk.at[level, my_half, :]
@@ -386,73 +426,83 @@
                 device_id_type=MESH,
             ).start()
 
+    def take_other(level):
+        @pl.when(bit_of(level) == 1)
+        def _():
+            piece = bk.at[level, other_half, :]
+            pltpu.make_async_copy(piece, piece, h_recv.at[level]).wait()
+
+    wide_cols = min(2 * TILE, toks)
+
+    def far(h, cols, levels, found):
+        rows = pl.ds(pl.multiple_of(h * HEAD_DIM, HEAD_DIM), HEAD_DIM)
+        query = q[h, cols, :]
+        for level in levels:
+            weight = lw[h, NEAR_LEVELS + level, :, cols]
+            weight = weight * (level_scale(NEAR_LEVELS + level) * SCALE)
+            found += dot_nt(bk[level, rows, :], query) * weight
+        return found
+
+    def finish(step, carry):
+        h = head_at(c, step)
+
+        @pl.when(me > 0)
+        def _():
+            pltpu.make_async_copy(vt.at[h], past_in.at[h], ps_recv.at[step]).wait()
+            pltpu.make_async_copy(stat_out.at[h], stat_in.at[h], ss_recv.at[step]).wait()
+
+        for start in range(0, toks, wide_cols):
+            cols = pl.ds(start, wide_cols)
+            own_top = own_stat[h, 0:1, cols]
+            past_top = stat_in[h, 0:1, cols]
+            top = jnp.maximum(own_top, past_top)
+            own_part = jnp.exp2(own_top - top)
+            past_part = jnp.exp2(past_top - top)
+            share = 1.0 / (own_part * own_stat[h, 1:2, cols] + past_part * stat_in[h, 1:2, cols])
+            found = acc[h, :, cols] + own_acc[h, :, cols] * (own_part * share)
+            found += past_in[h, :, cols].astype(F32) * (past_part * share)
+            found = far(h, cols, range(FAR_LEVELS), found)
+            mix[h, cols, :] = found.T.astype(BF16)
+        for there in range(groups):
+
+            @pl.when(zed != there)
+            def _():
+                pltpu.make_async_remote_copy(
+                    mix.at[h, pl.ds(there * out_rows, out_rows), :],
+                    tok.at[zed, h],
+                    o_send.at[step],
+                    o_recv.at[step],
+                    device_id={"heads": there},
+                    device_id_type=MESH,
+                ).start()
+
+        tok[zed, h] = mix[h, pl.ds(pl.multiple_of(zed * out_rows, out_rows), out_rows), :]
+        return carry
+
+    for level in range(1, FAR_LEVELS):
+        take(level)
+
     @pl.when(c == 1)
     def _():
         pltpu.make_async_copy(st, bk.at[0], z_recv).wait()
 
-    wide_cols = min(2 * TILE, toks)
-
-    def far(step):
-        h = head_at(c, step)
-
-        rows = pl.ds(pl.multiple_of(h * HEAD_DIM, HEAD_DIM), HEAD_DIM)
-        for start in range(0, toks, wide_cols):
-            cols = pl.ds(start, wide_cols)
-            query = q[h, cols, :]
-            found = acc[h, :, cols]
-            for level in range(FAR_LEVELS):
-                weight = lw[h, NEAR_LEVELS + level, :, cols]
-                weight = weight * (level_scale(NEAR_LEVELS + level) * SCALE)
-                found += dot_nt(bk[level, rows, :], query) * weight
-            mix[h, cols, :] = found.T.astype(BF16)
-        for hop in (4, 3, 5, 2, 6, 1, 7):
-            there = lax.rem(zed + hop, groups)
-            pltpu.make_async_remote_copy(
-                mix.at[h, pl.ds(pl.multiple_of(there * out_rows, out_rows), out_rows), :],
-                tok.at[zed * heads + h],
-                o_send.at[step],
-                o_recv.at[step],
-                device_id={"heads": there},
-                device_id_type=MESH,
-            ).start()
-        tok[zed * heads + h] = mix[h, pl.ds(pl.multiple_of(zed * out_rows, out_rows), out_rows), :]
-
     @pl.when(zed < groups - 1)
     def _():
         pl.semaphore_wait(here_sem, groups - 1 - zed)
 
-    def first(step, carry):
-        far(step)
-        return carry
-
-    lax.fori_loop(0, heads // 2, first, 0)
-
-    def second(step, carry):
-        window(step)
-
-        @pl.when(step == heads // 2)
-        def _():
-            for level in range(1, FAR_LEVELS):
-
-                @pl.when(bit_of(level) == 1)
-                def _():
-                    piece = bk.at[level, other_half, :]
-                    pltpu.make_async_copy(piece, piece, h_recv.at[level]).wait()
-
-        far(step)
-        return carry
-
-    lax.fori_loop(heads // 2, heads, second, 0)
+    lax.fori_loop(0, heads // 2, finish, 0)
+    for level in range(1, FAR_LEVELS):
+        take_other(level)
+    lax.fori_loop(heads // 2, heads, finish, 0)
 
     lanes = jnp.zeros((out_rows, HEAD_DIM), F32)
     for step in range(heads):
-        piece = tok.at[pl.ds(0, groups - 1)]
+        piece = tok.at[0:groups - 1, 0]
         pltpu.make_async_copy(piece, piece, o_recv.at[step]).wait()
         h = head_at(c, step)
         for group in range(groups):
-            index = group * heads + h
-            cols = pl.ds(pl.multiple_of(index * HEAD_DIM, HEAD_DIM), HEAD_DIM)
-            gated = tok[index].astype(F32) * silu[:, cols]
+            cols = pl.ds(pl.multiple_of((group * heads + h) * HEAD_DIM, HEAD_DIM), HEAD_DIM)
+            gated = tok[group, h].astype(F32) * silu[:, cols]
             silu[:, cols] = gated
             lanes += gated * gated
     square = jnp.sum(lanes, axis=1, keepdims=True) * (1.0 / (groups * heads * HEAD_DIM))
@@ -469,9 +519,17 @@
         pltpu.make_async_copy(st, st, z_send).wait()
 
     for step in range(heads):
-        pltpu.make_async_copy(k.at[0], k.at[0], ks_send.at[step]).wait()
-        pltpu.make_async_copy(vt.at[0], vt.at[0], vs_send.at[step]).wait()
-        piece = tok.at[pl.ds(0, groups - 1)]
+
+        @pl.when(me > 0)
+        def _():
+            pltpu.make_async_copy(q.at[0], q.at[0], qs_send.at[step]).wait()
+
+        @pl.when(me < seq_n - 1)
+        def _():
+            pltpu.make_async_copy(vt.at[0], vt.at[0], ps_send.at[step]).wait()
+            pltpu.make_async_copy(stat_out.at[0], stat_out.at[0], ss_send.at[step]).wait()
+
+        piece = tok.at[0 : groups - 1, 0]
         pltpu.make_async_copy(piece, piece, o_send.at[step]).wait()
     piece = tbuf.at[pl.ds(0, rows_x - 1)]
     pltpu.make_async_copy(piece, piece, t_send).wait()
@@ -504,6 +562,7 @@
     out_rows, model = gate_branch.shape
     row_n = rows_y * 2
     part = heads * HEAD_DIM // row_n
+    arrays = [queries, key_vectors, values, level_weights, gate_branch, norm_gain.reshape(1, -1)]
     dma = pltpu.SemaphoreType.DMA
     hbm = pl.BlockSpec(memory_space=pl.ANY)
     vmem = pl.BlockSpec(memory_space=pltpu.VMEM)
@@ -521,12 +580,17 @@
             pltpu.VMEM(turned_shape, BF16),
             pltpu.VMEM(head_shape, BF16),
             pltpu.VMEM(turned_shape, BF16),
+            pltpu.VMEM(turned_shape, BF16),
+            pltpu.VMEM((heads, 2, toks), F32),
+            pltpu.VMEM((heads, 2, toks), F32),
+            pltpu.VMEM(turned_shape, F32),
+            pltpu.VMEM((heads, 2, toks), F32),
             pltpu.VMEM((heads, level_weights.shape[0], 1, toks), F32),
             pltpu.VMEM(gate_branch.shape, BF16),
             pltpu.VMEM(gate_branch.shape, F32),
             pltpu.VMEM(turned_shape, F32),
             pltpu.VMEM(head_shape, BF16),
-            pltpu.VMEM((groups * heads, out_rows, HEAD_DIM), BF16),
+            pltpu.VMEM((groups, heads, out_rows, HEAD_DIM), BF16),
             pltpu.VMEM((heads * HEAD_DIM, HEAD_DIM), BF16),
             pltpu.VMEM((row_n, part, HEAD_DIM), BF16),
             pltpu.VMEM((row_n // 2 - 1, part, HEAD_DIM), BF16),
@@ -549,6 +613,8 @@
             dma((heads,)),
             dma((heads,)),
             dma((heads,)),
+            dma((heads,)),
+            dma((heads,)),
             dma,
             dma,
             dma((FAR_LEVELS,)),
@@ -560,10 +626,10 @@
             pltpu.SemaphoreType.REGULAR,
         ],
         compiler_params=pltpu.CompilerParams(
-            collective_id=0, has_side_effects=True, vmem_limit_bytes=67043328
+            collective_id=0, has_side_effects=True, vmem_limit_bytes=24 << 20
         ),
         name="layer",
-    )(queries, key_vectors, values, level_weights, gate_branch, norm_gain.reshape(1, -1))
+    )(*[pltpu.with_memory_space_constraint(array, pltpu.HBM) for array in arrays])
 
 
 def solution(mesh):

time: 48.4 us -> 45.1 us (0.932)
  the two profiles are of different devices: /device:TPU:3 before, /device:TPU:6 now
where the time goes in v3:
time: 45.1 us; the launch traced here: 44.8 us
  Pallas kernels  44 us (98%)
  local copies, waits for them, and re-layouts  0.8 us (2%)
    pallas_call x1, Pallas kernels, local(): pl.pallas_call(functools.partial(kernel, rows_x, rows_y, groups), out_sha...  44 us

profile of v3, /device:TPU:6, one launch (start us, length us, event | category | flops | bytes accessed | tf_op | source)
XLA Modules:
  0.0 44.8 jit_solution(11069704262637388602)
XLA Ops:
  0.0 44.0 %layer.1 = bf16[64,4096]{1,0:T(8,128)(2,1)S(1)} custom-call(bf16[512,512]{1,0:T(8,128)(2,1)} %q_hbm.1, bf16[512,512]{1,0:T(8,128)(2,1)} %k_hbm.1, bf16[512,512]{1,0:T(8,128)(2,1)} %v_hbm.1, f32[16,4,512]{2,1,0:T(4,128)} %lw_hbm.1, bf16[64,4096]{1,0:T(8,128)(2,1)} %gate_hbm.1, f32[1,4096]{1,0:T(1,128)} %bitcast.1), custom_call_target="tpu_custom_call" | custom-call | tf_op jit(solution)/shard_map/layer/pallas_call | solution.py:571
  44.0 0.8 %copy.8 = bf16[64,4096]{1,0:T(8,128)(2,1)} copy(bf16[64,4096]{1,0:T(8,128)(2,1)S(1)} %layer.1) | data formatting | bytes 1048576

commit v4 on v3

--- a/solution.py
+++ b/solution.py
@@ -61,6 +61,8 @@
     mix,
     tok,
     st,
+    sib,
+    chip,
     gat,
     bsrc,
     tsrc,
@@ -74,6 +76,8 @@
     lw_sem,
     gate_sem,
     gain_sem,
+    s_send,
+    s_recv,
     a_send,
     a_recv,
     z_send,
@@ -112,6 +116,9 @@
     def head_at(core, step):
         return lax.rem(core * (heads // 2) + step, heads)
 
+    def bit_of(level):
+        return lax.rem(me // (1 << level), 2)
+
     def row_id(place):
         return x * row_n + place
 
@@ -125,11 +132,11 @@
                 barrier, inc=1, device_id={"seq": me + apart}, device_id_type=MESH
             )
 
-    for step in range(1, row_n):
+    for step in (4, 3, 5, 2, 6, 1, 7):
         pl.semaphore_signal(
             barrier,
             inc=1,
-            device_id={"seq": row_id(lax.rem(r + step, row_n))},
+            device_id={"seq": row_id(lax.rem(y + step, rows_y) * 2 + c)},
             device_id_type=MESH,
         )
         greeted += 1
@@ -171,9 +178,9 @@
     for h in range(heads):
         pltpu.make_async_copy(k_hbm.at[:, pl.ds(0, HEAD_DIM)], k.at[h], k_sem.at[h]).wait()
         pltpu.make_async_copy(v_hbm.at[:, pl.ds(0, HEAD_DIM)], v.at[h], v_sem.at[h]).wait()
-        turned = v[h].T
-        vt[h] = turned
-        st[pl.ds(h * HEAD_DIM, HEAD_DIM), :] = dot_nn(turned, k[h]).astype(BF16)
+        st[pl.ds(h * HEAD_DIM, HEAD_DIM), :] = lax.dot_general(
+            v[h], k[h], (((0,), (0,)), ((), ())), preferred_element_type=F32
+        ).astype(BF16)
 
     pl.semaphore_wait(barrier, greeted + zed)
     for step in range(1, groups):
@@ -185,27 +192,13 @@
             )
 
 
-    for step in sorted(range(1, row_n), key=lambda step: abs(step - row_n // 2)):
-        place = lax.rem(r + step, row_n)
-        rows = pl.multiple_of(lax.rem(place, 2) * half + (place // 2) * part, part)
-        pltpu.make_async_remote_copy(
-            st.at[pl.ds(rows, part), :],
-            gat.at[r],
-            a_send,
-            a_recv,
-            device_id={"seq": row_id(place)},
-            device_id_type=MESH,
-        ).start()
+    sibling = me + 1 - 2 * c
     mine = pl.multiple_of(c * half + y * part, part)
-    gat[r] = st[pl.ds(mine, part), :]
-
-    sibling = me + 1 - 2 * c
-
-    @pl.when(c == 0)
-    def _():
-        pltpu.make_async_remote_copy(
-            st, bk.at[0], z_send, z_recv, device_id={"seq": sibling}, device_id_type=MESH
-        ).start()
+    my_half = pl.ds(pl.multiple_of(c * half, half), half)
+    other_half = pl.ds(pl.multiple_of((1 - c) * half, half), half)
+    pltpu.make_async_remote_copy(
+        st.at[other_half, :], sib, s_send, s_recv, device_id={"seq": sibling}, device_id_type=MESH
+    ).start()
 
     def send_queries(step):
         h = head_at(c, step)
@@ -223,8 +216,13 @@
 
     for h in range(heads):
         pltpu.make_async_copy(q_hbm.at[:, pl.ds(0, HEAD_DIM)], q.at[h], q_sem.at[h]).wait()
-    for step in range(heads - 1):
-        send_queries(step)
+    send_queries(0)
+
+    @pl.when(c == 0)
+    def _():
+        pltpu.make_async_remote_copy(
+            st, bk.at[0], z_send, z_recv, device_id={"seq": sibling}, device_id_type=MESH
+        ).start()
 
     @pl.when(me == 0)
     def _():
@@ -234,9 +232,6 @@
     @pl.when(c == 0)
     def _():
         bk[0] = jnp.zeros(bk.shape[1:], BF16)
-
-    def bit_of(level):
-        return lax.rem(me // (1 << level), 2)
 
     for level in range(1, FAR_LEVELS):
 
@@ -248,6 +243,33 @@
     gain_copy.wait()
     wide = gate[...].astype(F32)
     silu[...] = wide * jax.nn.sigmoid(wide)
+
+    pltpu.make_async_copy(sib, sib, s_recv).wait()
+    chip[...] = (st[my_half, :].astype(F32) + sib[...].astype(F32)).astype(BF16)
+    for step in (4, 3, 5, 2, 6, 1, 7):
+        place = lax.rem(y + step, rows_y)
+        pltpu.make_async_remote_copy(
+            chip.at[pl.ds(pl.multiple_of(place * part, part), part), :],
+            gat.at[y],
+            a_send,
+            a_recv,
+            device_id={"seq": row_id(place * 2 + c)},
+            device_id_type=MESH,
+        ).start()
+
+    @pl.when(bit_of(1) == 0)
+    def _():
+        pltpu.make_async_remote_copy(
+            chip,
+            bk.at[1, my_half, :],
+            c_send.at[1],
+            c_recv.at[1],
+            device_id={"seq": me + 2},
+            device_id_type=MESH,
+        ).start()
+
+    gat[y] = chip[pl.ds(pl.multiple_of(y * part, part), part), :]
+    send_queries(1)
 
     for copy in lw_copies:
         copy.wait()
@@ -257,6 +279,7 @@
 
     def within(step, carry):
         h = head_at(c, step)
+        vt[h] = v[h].T
         causal = key_at <= query_at
         apart = key_at ^ query_at
         for i in range(tiles):
@@ -294,56 +317,6 @@
 
     lax.fori_loop(0, heads, within, 0)
 
-    pltpu.make_async_copy(
-        gat.at[pl.ds(0, row_n - 1)], gat.at[pl.ds(0, row_n - 1)], a_recv
-    ).wait()
-    sums = [gat[i].astype(F32) for i in range(row_n)]
-    level_sums = []
-    while len(sums) > 1:
-        sums = [sums[2 * i] + sums[2 * i + 1] for i in range(len(sums) // 2)]
-        level_sums.append(sums)
-    low_levels = len(level_sums) - 1
-    firsts = []
-    count = 0
-    for level_list in level_sums[:-1]:
-        firsts.append(count)
-        for i in range(0, len(level_list), 2):
-            bsrc[count] = level_list[i].astype(BF16)
-            count += 1
-    total = level_sums[-1][0]
-    tsrc[...] = total
-    tbuf[x] = total
-    for step in range(1, rows_x):
-        pltpu.make_async_remote_copy(
-            tsrc,
-            tbuf.at[x],
-            t_send,
-            t_recv,
-            device_id={"seq": lax.rem(x + step, rows_x) * row_n + r},
-            device_id_type=MESH,
-        ).start()
-    for level in range(low_levels, 0, -1):
-        for step in (4, 3, 5, 2, 6, 1, 7, 0):
-            place = lax.rem(y + step, rows_y)
-            src = bsrc.at[firsts[level - 1] + place // (1 << level)]
-            dst = bk.at[level, pl.ds(mine, part), :]
-
-            @pl.when(lax.rem(place // (1 << (level - 1)), 2) == 1)
-            def _():
-                if step == 0:
-                    pltpu.make_async_copy(src, dst, c_recv.at[level]).start()
-                else:
-                    pltpu.make_async_remote_copy(
-                        src,
-                        dst,
-                        c_send.at[level],
-                        c_recv.at[level],
-                        device_id={"seq": row_id(place * 2 + c)},
-                        device_id_type=MESH,
-                    ).start()
-
-    send_queries(heads - 1)
-
     def onward(step, carry):
         h = head_at(1 - c, step)
         pltpu.make_async_copy(q.at[h], qn.at[h], qs_recv.at[step]).wait()
@@ -378,6 +351,60 @@
             ).start()
         return carry
 
+    @pl.when(me < seq_n - 1)
+    def _():
+        onward(0, 0)
+
+    pltpu.make_async_copy(
+        gat.at[pl.ds(0, rows_y - 1)], gat.at[pl.ds(0, rows_y - 1)], a_recv
+    ).wait()
+    sums = [gat[i].astype(F32) for i in range(rows_y)]
+    level_sums = []
+    while len(sums) > 1:
+        sums = [sums[2 * i] + sums[2 * i + 1] for i in range(len(sums) // 2)]
+        level_sums.append(sums)
+    low_levels = len(level_sums)
+    firsts = {}
+    count = 0
+    for level, level_list in enumerate(level_sums[:-1], 2):
+        firsts[level] = count
+        for i in range(0, len(level_list), 2):
+            bsrc[count] = level_list[i].astype(BF16)
+            count += 1
+    total = level_sums[-1][0]
+    tsrc[...] = total
+    tbuf[x] = total
+    for step in range(1, rows_x):
+        pltpu.make_async_remote_copy(
+            tsrc,
+            tbuf.at[x],
+            t_send,
+            t_recv,
+            device_id={"seq": lax.rem(x + step, rows_x) * row_n + r},
+            device_id_type=MESH,
+        ).start()
+    for level in range(low_levels, 1, -1):
+        for step in (4, 3, 5, 2, 6, 1, 7, 0):
+            place = lax.rem(y + step, rows_y)
+            src = bsrc.at[firsts[level] + place // (1 << level)]
+            dst = bk.at[level, pl.ds(mine, part), :]
+
+            @pl.when(lax.rem(place // (1 << (level - 1)), 2) == 1)
+            def _():
+                if step == 0:
+                    pltpu.make_async_copy(src, dst, c_recv.at[level]).start()
+                else:
+                    pltpu.make_async_remote_copy(
+                        src,
+                        dst,
+                        c_send.at[level],
+                        c_recv.at[level],
+                        device_id={"seq": row_id(place * 2 + c)},
+                        device_id_type=MESH,
+                    ).start()
+
+    send_queries(2)
+
     pltpu.make_async_copy(
         tbuf.at[pl.ds(0, rows_x - 1)], tbuf.at[pl.ds(0, rows_x - 1)], t_recv
     ).wait()
@@ -404,13 +431,11 @@
                         device_id_type=MESH,
                     ).start()
 
+    send_queries(3)
+
     @pl.when(me < seq_n - 1)
     def _():
-        lax.fori_loop(0, heads, onward, 0)
-
-
-    my_half = pl.ds(pl.multiple_of(c * half, half), half)
-    other_half = pl.ds(pl.multiple_of((1 - c) * half, half), half)
+        lax.fori_loop(1, heads - 1, onward, 0)
 
     def take(level):
         @pl.when(bit_of(level) == 1)
@@ -491,6 +516,11 @@
         pl.semaphore_wait(here_sem, groups - 1 - zed)
 
     lax.fori_loop(0, heads // 2, finish, 0)
+
+    @pl.when(me < seq_n - 1)
+    def _():
+        onward(heads - 1, 0)
+
     for level in range(1, FAR_LEVELS):
         take_other(level)
     lax.fori_loop(heads // 2, heads, finish, 0)
@@ -511,8 +541,9 @@
         cols = pl.ds(index * HEAD_DIM, HEAD_DIM)
         out_ref[:, cols] = (gain_ref[:, cols] * silu[:, cols] * inverse).astype(BF16)
 
-    piece = gat.at[pl.ds(0, row_n - 1)]
+    piece = gat.at[pl.ds(0, rows_y - 1)]
     pltpu.make_async_copy(piece, piece, a_send).wait()
+    pltpu.make_async_copy(sib, sib, s_send).wait()
 
     @pl.when(c == 0)
     def _():
@@ -534,7 +565,13 @@
     piece = tbuf.at[pl.ds(0, rows_x - 1)]
     pltpu.make_async_copy(piece, piece, t_send).wait()
     for level in range(1, FAR_LEVELS):
-        if level <= low_levels:
+        if level == 1:
+
+            @pl.when(bit_of(level) == 0)
+            def _():
+                pltpu.make_async_copy(chip, chip, c_send.at[level]).wait()
+
+        elif level <= low_levels:
             for own_bit in range(2):
 
                 @pl.when(bit_of(level) == own_bit)
@@ -592,8 +629,10 @@
             pltpu.VMEM(head_shape, BF16),
             pltpu.VMEM((groups, heads, out_rows, HEAD_DIM), BF16),
             pltpu.VMEM((heads * HEAD_DIM, HEAD_DIM), BF16),
-            pltpu.VMEM((row_n, part, HEAD_DIM), BF16),
-            pltpu.VMEM((row_n // 2 - 1, part, HEAD_DIM), BF16),
+            pltpu.VMEM((heads * HEAD_DIM // 2, HEAD_DIM), BF16),
+            pltpu.VMEM((heads * HEAD_DIM // 2, HEAD_DIM), BF16),
+            pltpu.VMEM((rows_y, part, HEAD_DIM), BF16),
+            pltpu.VMEM((rows_y // 2 - 1, part, HEAD_DIM), BF16),
             pltpu.VMEM((part, HEAD_DIM), F32),
             pltpu.VMEM((rows_x, part, HEAD_DIM), F32),
             pltpu.VMEM((2, part, HEAD_DIM), BF16),
@@ -603,6 +642,8 @@
             dma((heads,)),
             dma((heads,)),
             dma((heads,)),
+            dma,
+            dma,
             dma,
             dma,
             dma,

time: 45.1 us -> 43.1 us (0.956)
  Pallas kernels: 44 us -> 42.2 us
    pallas_call x1, Pallas kernels: 44 us -> 42.2 us  [local(): pl.pallas_call(functools.partial(kernel, rows_x, rows_y, groups), out_sha...]
where the time goes in v4:
time: 43.1 us; the launch traced here: 43 us
  Pallas kernels  42.2 us (98%)
  local copies, waits for them, and re-layouts  0.8 us (2%)
    pallas_call x1, Pallas kernels, local(): pl.pallas_call(functools.partial(kernel, rows_x, rows_y, groups), out_sha...  42.2 us

profile of v4, /device:TPU:6, one launch (start us, length us, event | category | flops | bytes accessed | tf_op | source)
XLA Modules:
  0.0 43.0 jit_solution(6171227546054035317)
XLA Ops:
  0.0 42.2 %layer.1 = bf16[64,4096]{1,0:T(8,128)(2,1)S(1)} custom-call(bf16[512,512]{1,0:T(8,128)(2,1)} %q_hbm.1, bf16[512,512]{1,0:T(8,128)(2,1)} %k_hbm.1, bf16[512,512]{1,0:T(8,128)(2,1)} %v_hbm.1, f32[16,4,512]{2,1,0:T(4,128)} %lw_hbm.1, bf16[64,4096]{1,0:T(8,128)(2,1)} %gate_hbm.1, f32[1,4096]{1,0:T(1,128)} %bitcast.1), custom_call_target="tpu_custom_call" | custom-call | tf_op jit(solution)/shard_map/layer/pallas_call | solution.py:608
  42.2 0.8 %copy.8 = bf16[64,4096]{1,0:T(8,128)(2,1)} copy(bf16[64,4096]{1,0:T(8,128)(2,1)S(1)} %layer.1) | data formatting | bytes 1048576

commit v5 on v4

--- a/solution.py
+++ b/solution.py
@@ -488,18 +488,18 @@
             found += past_in[h, :, cols].astype(F32) * (past_part * share)
             found = far(h, cols, range(FAR_LEVELS), found)
             mix[h, cols, :] = found.T.astype(BF16)
-        for there in range(groups):
-
-            @pl.when(zed != there)
-            def _():
-                pltpu.make_async_remote_copy(
-                    mix.at[h, pl.ds(there * out_rows, out_rows), :],
-                    tok.at[zed, h],
-                    o_send.at[step],
-                    o_recv.at[step],
-                    device_id={"heads": there},
-                    device_id_type=MESH,
-                ).start()
+            for there in range(start // out_rows, (start + wide_cols) // out_rows):
+
+                @pl.when(zed != there)
+                def _():
+                    pltpu.make_async_remote_copy(
+                        mix.at[h, pl.ds(there * out_rows, out_rows), :],
+                        tok.at[zed, h],
+                        o_send.at[step],
+                        o_recv.at[step],
+                        device_id={"heads": there},
+                        device_id_type=MESH,
+                    ).start()
 
         tok[zed, h] = mix[h, pl.ds(pl.multiple_of(zed * out_rows, out_rows), out_rows), :]
         return carry

time: 43.1 us -> 43 us (level)
  no operation moved by 1% of the time
where the time goes in v5:
time: 43 us; the launch traced here: 42.9 us
  Pallas kernels  42.1 us (98%)
  local copies, waits for them, and re-layouts  0.8 us (2%)
    pallas_call x1, Pallas kernels, local(): pl.pallas_call(functools.partial(kernel, rows_x, rows_y, groups), out_sha...  42.1 us

profile of v5, /device:TPU:6, one launch (start us, length us, event | category | flops | bytes accessed | tf_op | source)
XLA Modules:
  0.0 42.9 jit_solution(7707925988600212538)
XLA Ops:
  0.0 42.1 %layer.1 = bf16[64,4096]{1,0:T(8,128)(2,1)S(1)} custom-call(bf16[512,512]{1,0:T(8,128)(2,1)} %q_hbm.1, bf16[512,512]{1,0:T(8,128)(2,1)} %k_hbm.1, bf16[512,512]{1,0:T(8,128)(2,1)} %v_hbm.1, f32[16,4,512]{2,1,0:T(4,128)} %lw_hbm.1, bf16[64,4096]{1,0:T(8,128)(2,1)} %gate_hbm.1, f32[1,4096]{1,0:T(1,128)} %bitcast.1), custom_call_target="tpu_custom_call" | custom-call | tf_op jit(solution)/shard_map/layer/pallas_call | solution.py:608
  42.1 0.8 %copy.8 = bf16[64,4096]{1,0:T(8,128)(2,1)} copy(bf16[64,4096]{1,0:T(8,128)(2,1)S(1)} %layer.1) | data formatting | bytes 1048576

commit v6 on v5

--- a/solution.py
+++ b/solution.py
@@ -351,7 +351,7 @@
             ).start()
         return carry
 
-    @pl.when(me < seq_n - 1)
+    @pl.when(r < row_n - 1)
     def _():
         onward(0, 0)
 
@@ -405,6 +405,10 @@
 
     send_queries(2)
 
+    @pl.when((r == row_n - 1) & (me < seq_n - 1))
+    def _():
+        onward(0, 0)
+
     pltpu.make_async_copy(
         tbuf.at[pl.ds(0, rows_x - 1)], tbuf.at[pl.ds(0, rows_x - 1)], t_recv
     ).wait()
@@ -468,7 +472,7 @@
             found += dot_nt(bk[level, rows, :], query) * weight
         return found
 
-    def finish(step, carry):
+    def gather(step):
         h = head_at(c, step)
 
         @pl.when(me > 0)
@@ -486,7 +490,13 @@
             share = 1.0 / (own_part * own_stat[h, 1:2, cols] + past_part * stat_in[h, 1:2, cols])
             found = acc[h, :, cols] + own_acc[h, :, cols] * (own_part * share)
             found += past_in[h, :, cols].astype(F32) * (past_part * share)
-            found = far(h, cols, range(FAR_LEVELS), found)
+            acc[h, :, cols] = far(h, cols, range(low_levels + 1), found)
+
+    def finish(step):
+        h = head_at(c, step)
+        for start in range(0, toks, wide_cols):
+            cols = pl.ds(start, wide_cols)
+            found = far(h, cols, range(low_levels + 1, FAR_LEVELS), acc[h, :, cols])
             mix[h, cols, :] = found.T.astype(BF16)
             for there in range(start // out_rows, (start + wide_cols) // out_rows):
 
@@ -502,20 +512,28 @@
                     ).start()
 
         tok[zed, h] = mix[h, pl.ds(pl.multiple_of(zed * out_rows, out_rows), out_rows), :]
+
+    def whole(step, carry):
+        gather(step)
+        finish(step)
         return carry
 
-    for level in range(1, FAR_LEVELS):
+    @pl.when(zed < groups - 1)
+    def _():
+        pl.semaphore_wait(here_sem, groups - 1 - zed)
+
+    for level in range(1, low_levels + 1):
         take(level)
 
     @pl.when(c == 1)
     def _():
         pltpu.make_async_copy(st, bk.at[0], z_recv).wait()
 
-    @pl.when(zed < groups - 1)
-    def _():
-        pl.semaphore_wait(here_sem, groups - 1 - zed)
-
-    lax.fori_loop(0, heads // 2, finish, 0)
+    gather(0)
+    for level in range(low_levels + 1, FAR_LEVELS):
+        take(level)
+    finish(0)
+    lax.fori_loop(1, heads // 2, whole, 0)
 
     @pl.when(me < seq_n - 1)
     def _():
@@ -523,7 +541,7 @@
 
     for level in range(1, FAR_LEVELS):
         take_other(level)
-    lax.fori_loop(heads // 2, heads, finish, 0)
+    lax.fori_loop(heads // 2, heads, whole, 0)
 
     lanes = jnp.zeros((out_rows, HEAD_DIM), F32)
     for step in range(heads):

time: 43 us -> 43.1 us (level)
  no operation moved by 1% of the time
where the time goes in v6:
time: 43.1 us; the launch traced here: 43 us
  Pallas kernels  42.2 us (98%)
  local copies, waits for them, and re-layouts  0.8 us (2%)
    pallas_call x1, Pallas kernels, local(): pl.pallas_call(functools.partial(kernel, rows_x, rows_y, groups), out_sha...  42.2 us

profile of v6, /device:TPU:6, one launch (start us, length us, event | category | flops | bytes accessed | tf_op | source)
XLA Modules:
  0.0 43.0 jit_solution(12138774008289035532)
XLA Ops:
  0.0 42.2 %layer.1 = bf16[64,4096]{1,0:T(8,128)(2,1)S(1)} custom-call(bf16[512,512]{1,0:T(8,128)(2,1)} %q_hbm.1, bf16[512,512]{1,0:T(8,128)(2,1)} %k_hbm.1, bf16[512,512]{1,0:T(8,128)(2,1)} %v_hbm.1, f32[16,4,512]{2,1,0:T(4,128)} %lw_hbm.1, bf16[64,4096]{1,0:T(8,128)(2,1)} %gate_hbm.1, f32[1,4096]{1,0:T(1,128)} %bitcast.1), custom_call_target="tpu_custom_call" | custom-call | tf_op jit(solution)/shard_map/layer/pallas_call | solution.py:626
  42.2 0.8 %copy.8 = bf16[64,4096]{1,0:T(8,128)(2,1)} copy(bf16[64,4096]{1,0:T(8,128)(2,1)S(1)} %layer.1) | data formatting | bytes 1048576
